TPU v7x, 32 devices: a whole 2x2x4 slice. The times are simulated.
32 devices in a mesh: row: 4 (over y, core), col: 8 (over z, x).
Axes of the slice: x: 2, y: 2, z: 4, core: 2. Of those that a mesh axis runs over, the one named last changes fastest.
Arguments:
- integrals: bfloat16 [4, 8, 32, 512, 512], P('row', 'col'), may hold values from -0.0625 to 0.0625
- tile_count: int32 [4, 8], P('row', 'col'), may hold values from 1 to 32, as said below
- tile_list: int32 [4, 8, 32], P('row', 'col'), may hold values from 0 to 31, as said below
- amplitudes: bfloat16 [32, 512, 1024], P('col', 'row'), may hold values from -6 to 6
- pair_energy: float32 [16384], P(('row', 'col')), may hold values from 1 to 4
- occ_energy: float32 [32], replicated, may hold values from -1.5 to -0.25
- partner: int32 [16384], P(('row', 'col')), may hold values from 0 to 16383, as said below
Outputs:
- amp_update: float32 [16384, 1024], P(('row', 'col'))
Inputs may be any that keep to these rules, and one draw needn't show every extreme that they name: `tile_count`: some grid cell holds exactly 32 live tiles. `tile_list`: each grid cell's list is a permutation of 0 to 31; only its first tile_count entries name live tiles. partner is an involution. Numbering the rows in consecutive blocks of 512, the rows of one block have their partners among the 8 blocks of the same aligned group of 4096 rows, exactly 64 of them in each of these blocks.
All inputs are finite; a program needn't handle non-finite values.
Results may differ from a plain program's by a relative error of at most 0.0003.
Values may be sent and summed in bfloat16 or wider, within the bound.
A program may use at most 128 MiB of HBM per device.

v0:
```python
import jax
import jax.numpy as jnp
from jax import lax
from jax.sharding import PartitionSpec as P

slot_batch = 4


def add_tiles(partial_value, tile_data, blocks, last_slot, amp_blocks):
    nblock_col = amp_blocks.shape[0]
    slot_total = tile_data.shape[0]
    turn_count = (last_slot + slot_batch - 1) // slot_batch

    def one_turn(turn_no, running):
        slot_index = turn_no * slot_batch + jnp.arange(slot_batch, dtype=jnp.int32)
        is_live = slot_index < last_slot
        clipped = jnp.clip(slot_index, 0, slot_total - 1)
        chosen = jnp.take(tile_data, clipped, axis=0)
        position = jnp.take(blocks, clipped, axis=0)
        block_row = position // nblock_col
        block_col = position % nblock_col
        operand = jnp.take(amp_blocks, block_col, axis=0)
        product = jnp.einsum("uab,ubo->uao", chosen, operand, preferred_element_type=jnp.float32)
        product = product * is_live.astype(jnp.float32)[:, None, None]
        for member in range(slot_batch):
            current = lax.dynamic_index_in_dim(running, block_row[member], 0, keepdims=False)
            running = lax.dynamic_update_index_in_dim(
                running, current + product[member], block_row[member], 0
            )
        return running

    return lax.fori_loop(0, turn_count, one_turn, partial_value)


def swap_occupied(rows, occ_count):
    shaped = rows.reshape(rows.shape[0], occ_count, occ_count)
    return jnp.swapaxes(shaped, 1, 2).reshape(rows.shape)


def body(integrals, tile_count, tile_list, amplitudes, pair_energy, occ_energy, partner):
    tile_data = integrals[0, 0]
    blocks = tile_list[0, 0]
    own_count = tile_count[0, 0]
    slots = blocks.shape[0]
    gathered = lax.all_gather(amplitudes, "row", axis=1, tiled=True)
    nblock_col, tile_width, occ_pairs = gathered.shape
    nblock_row = slots // nblock_col
    partial_value = jnp.zeros((nblock_row, tile_width, occ_pairs), jnp.float32)
    partial_value = add_tiles(partial_value, tile_data, blocks, own_count, gathered)
    flat_rows = partial_value.reshape(nblock_row * tile_width, occ_pairs)
    occ_count = occ_energy.shape[0]
    rows_total = flat_rows.shape[0]
    group_map = lax.all_gather(partner, "col", axis=0, tiled=True)
    local_map = group_map % rows_total
    operand = flat_rows + swap_occupied(jnp.take(flat_rows, local_map, axis=0), occ_count)
    symmetric = lax.psum_scatter(operand, "col", scatter_dimension=0, tiled=True)
    denominator = pair_energy[:, None] - (occ_energy[:, None] + occ_energy[None, :]).reshape(
        1, occ_pairs
    )
    return symmetric / denominator


def solution(mesh):
    return jax.shard_map(
        body,
        mesh=mesh,
        in_specs=(
            P("row", "col", None, None, None),
            P("row", "col"),
            P("row", "col", None),
            P("col", "row", None),
            P(("row", "col")),
            P(),
            P(("row", "col")),
        ),
        out_specs=P(("row", "col"), None),
        check_vma=False,
    )
```

profile of v0, /device:TPU:0, one launch (start us, length us, event | category | flops | bytes accessed | tf_op | source)
XLA Modules:
  0.0 762.7 jit_solution(15672518630348271505)
XLA Ops:
  8.0 28.1 %all-gather = s32[8,1,512]{2,1,0:T(1,128)S(1)} all-gather(s32[1,1,512]{2,1,0:T(1,128)} %bitcast.45), channel_id=1, replica_groups=mesh['row'=4,'col'=8] {'col'}, dimensions={0}, use_global_device_ids=true | all-gather | bytes 18432 | tf_op jit(solution)/shard_map/all_gather | solution.py:53
  36.1 10.0 %all-gather.3.cloned.1.call-done = bf16[4,512,1024]{2,1,0:T(8,128)(2,1)} async-done(((bf16[4,128,1024]{2,1,0:T(8,128)(2,1)}), bf16[4,512,1024]{2,1,0:T(8,128)(2,1)}) %all-gather.3.cloned.1.call-update) | async-done | bytes 4194320 | tf_op jit(solution)/shard_map/all_gather | solution.py:45
  46.1 7.9 %broadcast_in_dim.58 = f32[8,512,1024]{2,1,0:T(8,128)} broadcast(f32[]{:T(128)} %constant.172.clone.1), dimensions={} | broadcast | bytes 16777220 | tf_op jit(solution)/shard_map/broadcast_in_dim | solution.py:48
  54.0 78.4 %while.12 = (s32[]{:T(128)}, f32[8,512,1024]{2,1,0:T(8,128)}, s32[]{:T(128)}, s32[32]{0:T(128)S(1)}, bf16[32,512,512]{2,1,0:T(8,128)(2,1)}, /*index=5*/bf16[4,51...) while((s32[]{:T(128)}, f32[8,512,1024]{2,1,0:T(8,128)}, ...), condition=%wide.region_1.2_spmd, body=%wide.region_0.1_spmd.sunk | while | flops 2154825984 | bytes 52437604 | solution.py:32
  63.9 6.5 gather_fusion.2
  70.4 5.0 gather_fusion.1
  75.3 4.6 broadcast_multiply_fusion.2
  80.0 3.3 fusion.33
  83.3 3.3 fusion.34
  86.6 3.3 fusion.35
  89.9 3.3 fusion.36
  103.1 6.5 gather_fusion.2
  109.6 5.0 gather_fusion.1
  114.6 4.6 broadcast_multiply_fusion.2
  119.2 3.3 fusion.33
  122.5 3.3 fusion.34
  125.8 3.3 fusion.35
  132.4 28.1 %gather_fusion.3 = f32[4096,1024]{1,0:T(8,128)} fusion(f32[4096,1024]{1,0:T(8,128)} %bitcast.39, s32[4096]{0:T(1024)S(1)} %broadcast_clamp_fusion), kind=kCustom, calls=%fused_computation.3 | custom fusion | bytes 33570816 | tf_op jit(solution)/shard_map/jit(_take)/gather | solution.py:55
  160.5 17.5 %copy.12 = f32[4096,1024]{0,1:T(8,128)} copy(f32[4096,1024]{1,0:T(8,128)} %gather_fusion.3) | data formatting | bytes 33554432 | tf_op jit(solution)/shard_map/jit(_take)/gather | solution.py:55
  178.0 6.8 select_bitcast_fusion
  184.9 18.0 %copy.13 = f32[4096,32,32]{0,2,1:T(8,128)} copy(f32[4096,32,32]{0,1,2:T(8,128)S(1)} %select_bitcast_fusion) | data formatting | bytes 33554432 | tf_op jit(solution)/shard_map/transpose | solution.py:37
  202.9 17.5 %copy.14 = f32[4096,1024]{1,0:T(8,128)} copy(f32[4096,1024]{0,1:T(8,128)} %bitcast.41) | data formatting | bytes 33554432 | tf_op jit(solution)/shard_map/reshape | solution.py:37
  220.4 17.0 %bitcast_add_fusion = f32[4096,1024]{1,0:T(8,128)} fusion(f32[4096,1024]{1,0:T(8,128)} %copy.14, f32[8,512,1024]{2,1,0:T(8,128)} %get-tuple-element.100), kind=kLoop, calls=%fused_computation.54 | loop fusion | flops 4194304 | bytes 50331648 | tf_op jit(solution)/shard_map/add | solution.py:55
  238.2 514.5 %reduce-scatter.2.cloned.1.call-done = f32[512,1024]{1,0:T(8,128)} async-done(((f32[4096,1024]{1,0:T(8,128)}), f32[512,1024]{1,0:T(8,128)}) %reduce-scatter.2.cloned.1.call-update) | async-done | bytes 2097168 | tf_op jit(solution)/shard_map/reduce_scatter | solution.py:56
  (34 shorter events, 12.2 us)
Async XLA Ops:
  6.5 39.6 %all-gather.3.cloned.1.call-start = ((), (), s32[]{:S(2)}) async-start(), calls=%async_computation.1 | async-start | bytes 5242880 | tf_op jit(solution)/shard_map/all_gather | solution.py:45
  7.3 745.4 %reduce-scatter.2.cloned.1.call-start = ((), (), s32[]{:S(2)}) async-start(), calls=%async_computation.2 | async-start | bytes 18874368 | tf_op jit(solution)/shard_map/reduce_scatter | solution.py:56
  46.1 7.9 %copy-start = (s32[1,1,32]{2,1,0:T(1,128)S(1)}, s32[1,1,32]{2,1,0:T(1,128)}, u32[]{:S(2)}) copy-start(s32[1,1,32]{2,1,0:T(1,128)} %param.11) | copy-start | bytes 388
  237.4 0.7 copy-start.2
  237.4 515.3 %copy-start.1 = (f32[512]{0:T(512)S(1)}, f32[512]{0:T(512)}, u32[]{:S(2)}) copy-start(f32[512]{0:T(512)} %param.13) | copy-start | bytes 6148
Sparse Core Ops, SparseCore 0:
  8.9 37.1 all-gather.2
  237.5 515.0 reduce-scatter.1
where the time goes:
time: 766 us; the launch traced here: 763 us
  waiting for transfers between devices  525 us (69%)
  local copies, waits for them, and re-layouts  115 us (15%)
  other arithmetic  55.1 us (7%)
  blocking collectives  28.1 us (4%)
  loops' own time  15.8 us (2%)
  between operations  14.1 us (2%)
  matrix products  9.25 us (1%)
    reduce_scatter x1, waiting for transfers between devices, body(): lax.psum_scatter(operand, 'col', scatter_dimension=0, tiled=True)  514 us
    gather x2, local copies, waits for them, and re-layouts, body(): jnp.take(flat_rows, local_map, axis=0)  45.6 us
    all_gather x1, blocking collectives, body(): group_map = lax.all_gather(partner, 'col', axis=0, tiled=True)  28.1 us
    dynamic_update_slice x8, other arithmetic, one_turn(): lax.dynamic_update_index_in_dim(running, current + product[member], block...  26.5 us
    transpose x1, local copies, waits for them, and re-layouts, swap_occupied(): return jnp.swapaxes(shaped, 1, 2).reshape(rows.shape)  18 us
    reshape x1, local copies, waits for them, and re-layouts, swap_occupied(): return jnp.swapaxes(shaped, 1, 2).reshape(rows.shape)  17.5 us
    add x1, other arithmetic, body(): flat_rows + swap_occupied(jnp.take(flat_rows, local_map, axis=0), occ_count)  17 us
    another operation x1, loops' own time, add_tiles(): return lax.fori_loop(0, turn_count, one_turn, partial_value)  15.8 us
  transfers between devices with their start and end apart: 2, of which 2 were waited for; matrix products, arithmetic and copies ran while one was open for 0% of the time, Pallas kernels for 0%

commit v1 on v0

v1 whole, which is shorter than its diff:
```python
import functools

import jax
import jax.numpy as jnp
from jax import lax
from jax.experimental import pallas as pl
from jax.experimental.pallas import tpu as pltpu
from jax.sharding import PartitionSpec as P

MESH = pl.DeviceIdType.MESH
F32, BF16, I32, I16 = jnp.float32, jnp.bfloat16, jnp.int32, jnp.int16
LEVELS = 32767.0


def iota(shape, axis):
    return lax.broadcasted_iota(I32, shape, axis)


def row_places(partner, me, n):
    rows = partner.shape[0]
    half = rows // n // 2
    own = (n + 1) * half
    local = partner % (n * rows)
    block, within = local // rows, local % rows
    index = jnp.arange(rows, dtype=I32)
    key = jnp.where(block < me, within, index)
    before = (block[None, :] == block[:, None]) & (key[None, :] < key[:, None])
    rank = jnp.sum(before.astype(I32), axis=1)
    shift = (block - me + n) % n
    owned = jnp.where(me < block, rank < half, rank >= half)
    step = (shift - 1) * half + rank % half
    place = jnp.where(block == me, rank, jnp.where(owned, 2 * half + step, own + step))
    found = jnp.sum(jnp.where(index[None, :] == within[:, None], place[None, :], 0), axis=1)
    mirror = jnp.where(block == me, rows + found, -1)
    return place, mirror


def sort_kernel(n, half, occ, slot_ref, live_ref, tile_ref, place_ref, u_ref, w_ref, swap_ref):
    c, i = pl.program_id(0), pl.program_id(1)
    rows = place_ref.shape[2]
    tile = tile_ref.shape[3]
    own = (n + 1) * half
    live = live_ref[i * pl.num_programs(0) + c]

    @pl.when((c == 0) & (i == 0))
    def _():
        total = swap_ref.shape[0]
        chunk = 128

        @pl.loop(0, total // chunk)
        def _(k):
            x = iota((chunk, total), 0) + k * chunk
            y = iota((chunk, total), 1)
            hit = x == (y % occ) * occ + y // occ
            swap_ref[pl.ds(pl.multiple_of(k * chunk, chunk), chunk), :] = hit.astype(F32).astype(BF16)

    for j in range(tile // rows):
        o = i * (tile // rows) + j
        place = place_ref[o]
        hit = (iota((rows, rows), 0) == place) & (live > 0)
        one_hot = hit.astype(F32).astype(BF16)
        got = jnp.dot(one_hot, tile_ref[0, 0, 0, j * rows : (j + 1) * rows, :], preferred_element_type=F32)
        u_ref[o] = got[:own].astype(BF16)
        for d in range(1, n):
            a = lax.rem(o + d, n)
            start = (n - d - 1) * half
            w_ref[a, start : start + half, :] = got[own + (d - 1) * half : own + d * half].astype(BF16)


def reduce_kernel(
    n, half, u_hbm, w_hbm, t_hbm, swap_hbm, z_ref,
    ubuf, wbuf, tbuf, t2buf, swap, sbuf, qsend, ssend, qrecv, srecv, fbuf,
    usem, wsem, tsem, psem, qs, qr, ss, sr, xs, xr,
):
    me = lax.axis_index("col")
    depth, width = tbuf.shape
    own = (n + 1) * half
    chunks = n + 1

    load_t = pltpu.make_async_copy(t_hbm, tbuf, tsem)
    load_p = pltpu.make_async_copy(swap_hbm, swap, psem)
    load_t.start()
    load_p.start()

    def load(a):
        return (
            pltpu.make_async_copy(u_hbm.at[a], ubuf.at[a], usem.at[a]),
            pltpu.make_async_copy(w_hbm.at[a], wbuf.at[a], wsem.at[a]),
        )

    for step in range(n):
        for copy in load(lax.rem(me + 1 + step, n)):
            copy.start()

    barrier = pltpu.get_barrier_semaphore()
    for d in range(1, n):
        pl.semaphore_signal(barrier, inc=1, device_id={"col": lax.rem(me + d, n)}, device_id_type=MESH)
    pl.semaphore_wait(barrier, n - 1)

    load_t.wait()
    load_p.wait()
    high = 256

    @pl.loop(0, depth // high)
    def _(k):
        at = pl.ds(pl.multiple_of(k * high, high), high)
        for c in range(0, width, 256):
            t2buf[at, c : c + 256] = jnp.dot(tbuf[at, :], swap[:, c : c + 256], preferred_element_type=F32).astype(BF16)

    def product(a, out):
        for copy in load(a):
            copy.wait()

        @pl.loop(0, width // 256)
        def _(c):
            at = pl.ds(pl.multiple_of(c * 256, 256), 256)
            first = jnp.dot(ubuf[a], tbuf[:, at], preferred_element_type=F32)
            second = jnp.dot(wbuf[a], t2buf[:, at], preferred_element_type=F32)
            out[0 : 2 * half, at] = first[: 2 * half]
            out[2 * half : own, at] = first[2 * half :] + second

    def q_copy(a, source):
        return (
            pltpu.make_async_remote_copy(
                src_ref=qsend.at[a], dst_ref=qrecv.at[source], send_sem=qs.at[a], recv_sem=qr.at[source],
                device_id={"col": a}, device_id_type=MESH,
            ),
            pltpu.make_async_remote_copy(
                src_ref=ssend.at[a], dst_ref=srecv.at[source], send_sem=ss.at[a], recv_sem=sr.at[source],
                device_id={"col": a}, device_id_type=MESH,
            ),
        )

    diagonal = iota((half, 128), 0) == iota((half, 128), 1)

    @pl.loop(0, n - 1)
    def _(step):
        a = lax.rem(me + 1 + step, n)
        product(a, sbuf)
        for k in range(chunks):
            part = sbuf[k * half : (k + 1) * half, :]
            most = jnp.max(jnp.abs(part), axis=1, keepdims=True)
            scale = most * (1.0 / LEVELS)
            inverse = jnp.where(most > 1e-30, LEVELS / jnp.maximum(most, 1e-30), 0.0)
            level = jnp.round(part * inverse)
            qsend[a, k] = level.astype(I32).astype(I16)
            ssend[a, k : k + 1, :] = jnp.sum(jnp.where(diagonal, scale, 0.0), axis=0, keepdims=True)
        for copy in q_copy(a, me):
            copy.start()

    product(me, z_ref)

    @pl.loop(1, n)
    def _(d):
        source = lax.rem(me + n - d, n)
        for copy in q_copy(source, source):
            copy.wait_recv()
        for k in range(chunks):
            scale = jnp.sum(jnp.where(diagonal, srecv[source, k : k + 1, :], 0.0), axis=1, keepdims=True)
            z_ref[k * half : (k + 1) * half, :] += qrecv[source, k].astype(I32).astype(F32) * scale

    def x_copy(d):
        return pltpu.make_async_remote_copy(
            src_ref=z_ref.at[pl.ds((d + 1) * half, half)], dst_ref=fbuf.at[pl.ds((n - d - 1) * half, half)],
            send_sem=xs.at[d], recv_sem=xr.at[n - d],
            device_id={"col": lax.rem(me + d, n)}, device_id_type=MESH,
        )

    for d in range(1, n):
        x_copy(d).start()
    for d in range(1, n):
        x_copy(d).wait_recv()
    z_ref[own:, :] = fbuf[...]
    for d in range(1, n):
        x_copy(d).wait_send()

    @pl.loop(1, n)
    def _(d):
        for copy in q_copy(lax.rem(me + d, n), me):
            copy.wait_send()


def final_kernel(half, own, z_ref, swap_ref, place_ref, mirror_ref, pair_ref, occ_ref, out_ref, pieces):
    rows, width = z_ref.shape

    @pl.when(pl.program_id(0) == 0)
    def _():
        rest = z_ref[...]
        for p in range(3):
            piece = rest.astype(BF16)
            pieces[p] = piece
            rest = rest - piece.astype(F32)

    chunk = out_ref.shape[1]
    at = pl.ds(pl.multiple_of(pl.program_id(0) * chunk, chunk), chunk)
    place, mirror = place_ref[...], mirror_ref[...]

    def hot(count, first):
        number = iota((rows, count), 1) + first
        return ((number == place) | (number == mirror)).astype(F32).astype(BF16)

    hot_own, hot_far, hot_self = hot(own, 0), hot(rows - own, own), hot(2 * half, rows)
    mixer = swap_ref[...]
    total = None
    for p in (2, 1, 0):
        far = jnp.dot(pieces[p, own:, :], mixer, preferred_element_type=F32).astype(BF16)
        near = jnp.dot(pieces[p, : 2 * half, :], mixer, preferred_element_type=F32).astype(BF16)
        term = jnp.dot(hot_own, pieces[p, :own, at], preferred_element_type=F32)
        mine = jnp.dot(hot_self, near, preferred_element_type=F32)
        other = jnp.dot(hot_far, far, preferred_element_type=F32)
        term = term + (mine + other)
        total = term if total is None else total + term
    out_ref[...] = total / (pair_ref[...] - occ_ref[...])


def body(integrals, tile_count, tile_list, amplitudes, pair_energy, occ_energy, partner):
    n = lax.axis_size("col")
    me = lax.axis_index("col")
    rows = partner.shape[0]
    half = rows // n // 2
    own = (n + 1) * half
    slots, tile = integrals.shape[2], integrals.shape[3]
    bc, _, width = amplitudes.shape
    br = slots // bc
    occ = occ_energy.shape[0]
    depth = bc * tile

    place, mirror = row_places(partner, me, n)
    places = lax.all_gather(place, "col", axis=0, tiled=True).reshape(n, 1, rows)
    gathered = lax.all_gather(amplitudes, "row", axis=1, tiled=True).reshape(depth, width)

    number = jnp.arange(slots, dtype=I32)
    slot = jnp.sum(jnp.where(tile_list[0, 0][None, :] == number[:, None], number[None, :], 0), axis=1)
    live = (slot < tile_count[0, 0]).astype(I32)

    u, w, swap = pl.pallas_call(
        functools.partial(sort_kernel, n, half, occ),
        grid_spec=pltpu.PrefetchScalarGridSpec(
            num_scalar_prefetch=2,
            grid=(bc, br),
            in_specs=[
                pl.BlockSpec((1, 1, 1, tile, tile), lambda c, i, s, l: (0, 0, s[i * bc + c], 0, 0)),
                pl.BlockSpec((n, 1, rows), lambda c, i, s, l: (0, 0, 0)),
            ],
            out_specs=[
                pl.BlockSpec((n, own, tile), lambda c, i, s, l: (0, 0, c)),
                pl.BlockSpec((n, rows - own, tile), lambda c, i, s, l: (0, 0, c)),
                pl.BlockSpec((width, width), lambda c, i, s, l: (0, 0)),
            ],
        ),
        out_shape=[
            jax.ShapeDtypeStruct((n, own, depth), BF16),
            jax.ShapeDtypeStruct((n, rows - own, depth), BF16),
            jax.ShapeDtypeStruct((width, width), BF16),
        ],
        compiler_params=pltpu.CompilerParams(vmem_limit_bytes=40 * 1024 * 1024),
        cost_estimate=pl.CostEstimate(
            flops=2 * slots * rows * tile * tile, bytes_accessed=4 * slots * tile * tile, transcendentals=0
        ),
        name="sort_rows",
    )(slot, live, integrals, places)

    anywhere = pl.BlockSpec(memory_space=pl.ANY)
    scale_rows = -(-(n + 1) // 8) * 8
    dma = pltpu.SemaphoreType.DMA
    z = pl.pallas_call(
        functools.partial(reduce_kernel, n, half),
        out_shape=jax.ShapeDtypeStruct((rows, width), F32),
        in_specs=[anywhere] * 4,
        out_specs=pl.BlockSpec(memory_space=pltpu.VMEM),
        scratch_shapes=[
            pltpu.VMEM((n, own, depth), BF16),
            pltpu.VMEM((n, rows - own, depth), BF16),
            pltpu.VMEM((depth, width), BF16),
            pltpu.VMEM((depth, width), BF16),
            pltpu.VMEM((width, width), BF16),
            pltpu.VMEM((own, width), F32),
            pltpu.VMEM((n, n + 1, half, width), I16),
            pltpu.VMEM((n, scale_rows, 128), F32),
            pltpu.VMEM((n, n + 1, half, width), I16),
            pltpu.VMEM((n, scale_rows, 128), F32),
            pltpu.VMEM((rows - own, width), F32),
            dma((n,)), dma((n,)), dma, dma,
            dma((n,)), dma((n,)), dma((n,)), dma((n,)), dma((n,)), dma((n,)),
        ],
        compiler_params=pltpu.CompilerParams(
            collective_id=0, has_side_effects=True, vmem_limit_bytes=63 * 1024 * 1024
        ),
        name="reduce_pairs",
    )(u, w, gathered, swap)

    chunk = 256
    whole = lambda k: (0, 0)
    return pl.pallas_call(
        functools.partial(final_kernel, half, own),
        grid=(width // chunk,),
        in_specs=[
            pl.BlockSpec((rows, width), whole),
            pl.BlockSpec((width, chunk), lambda k: (0, k)),
            pl.BlockSpec((rows, 1), whole),
            pl.BlockSpec((rows, 1), whole),
            pl.BlockSpec((rows, 1), whole),
            pl.BlockSpec((1, chunk), lambda k: (0, k)),
        ],
        out_specs=pl.BlockSpec((rows, chunk), lambda k: (0, k)),
        out_shape=jax.ShapeDtypeStruct((rows, width), F32),
        scratch_shapes=[pltpu.VMEM((3, rows, width), BF16)],
        compiler_params=pltpu.CompilerParams(vmem_limit_bytes=40 * 1024 * 1024),
        name="finish_rows",
    )(
        z, swap, place[:, None], mirror[:, None], pair_energy[:, None],
        (occ_energy[:, None] + occ_energy[None, :]).reshape(1, width),
    )


def solution(mesh):
    return jax.shard_map(
        body,
        mesh=mesh,
        in_specs=(
            P("row", "col", None, None, None),
            P("row", "col"),
            P("row", "col", None),
            P("col", "row", None),
            P(("row", "col")),
            P(),
            P(("row", "col")),
        ),
        out_specs=P(("row", "col"), None),
        check_vma=False,
    )
```

time: 766 us -> 238 us (0.31)
  waiting for transfers between devices: 525 us -> 0.71 us
  Pallas kernels: 0 us -> 180 us
  local copies, waits for them, and re-layouts: 115 us -> 8.6 us
  other arithmetic: 55.1 us -> 2.9 us
  loops' own time: 15.8 us -> 0 us
  matrix products: 9.25 us -> 0 us
    reduce_scatter x1 -> x0, waiting for transfers between devices: 514 us -> none  [body(): lax.psum_scatter(operand, 'col', scatter_dimension=0, tiled=True)]
    pallas_call x0 -> x3, Pallas kernels: none -> 180 us  [the longest x1 140 us: body(): pl.pallas_call(functools.partial(reduce_kernel, n, half), out_shape=jax.S...]
    gather x8 -> x0, local copies, waits for them, and re-layouts: 69.7 us -> none  [the longest x2 45.6 us: body(): jnp.take(flat_rows, local_map, axis=0)]
    dynamic_update_slice x8 -> x0, other arithmetic: 26.5 us -> none  [one_turn(): lax.dynamic_update_index_in_dim(running, current + product[member], block...]
    transpose x1 -> x0, local copies, waits for them, and re-layouts: 18 us -> none  [swap_occupied(): return jnp.swapaxes(shaped, 1, 2).reshape(rows.shape)]
    reshape x1 -> x0, local copies, waits for them, and re-layouts: 17.5 us -> none  [swap_occupied(): return jnp.swapaxes(shaped, 1, 2).reshape(rows.shape)]
    add x1 -> x0, other arithmetic: 17 us -> none  [body(): flat_rows + swap_occupied(jnp.take(flat_rows, local_map, axis=0), occ_count)]
    another operation x1 -> x0, loops' own time: 15.8 us -> none  [add_tiles(): return lax.fori_loop(0, turn_count, one_turn, partial_value)]
  transfers between devices with their start and end apart: 2 -> 1, of which waited for: 2 -> 0; matrix products, arithmetic and copies ran while one was open for 0% -> 2% of each run, Pallas kernels for 0% -> 12%
where the time goes in v1:
time: 238 us; the launch traced here: 234 us
  Pallas kernels  180 us (76%)
  blocking collectives  27.9 us (12%)
  between operations  14.1 us (6%)
  local copies, waits for them, and re-layouts  8.6 us (4%)
  other arithmetic  2.9 us (1%)
    pallas_call x1, Pallas kernels, body(): pl.pallas_call(functools.partial(reduce_kernel, n, half), out_shape=jax.S...  140 us
    pallas_call x1, Pallas kernels, body(): pl.pallas_call(functools.partial(sort_kernel, n, half, occ), grid_spec=pl...  29.1 us
    all_gather x1, blocking collectives, body(): lax.all_gather(place, 'col', axis=0, tiled=True).reshape(n, 1, rows)  27.9 us
    pallas_call x1, Pallas kernels, body(): pl.pallas_call(functools.partial(final_kernel, half, own), grid=(width //...  11.2 us
    unnamed x8, local copies, waits for them, and re-layouts  7.39 us
  transfers between devices with their start and end apart: 1, of which 0 were waited for; matrix products, arithmetic and copies ran while one was open for 2% of the time, Pallas kernels for 12%

profile of v1, /device:TPU:0, one launch (start us, length us, event | category | flops | bytes accessed | tf_op | source)
XLA Modules:
  0.0 234.2 jit_solution(17502941409147946189)
XLA Ops:
  6.5 0.0 all-gather.3.cloned.1.call-start
  6.5 0.7 all-gather.3.cloned.1.call-update
  7.9 0.7 iota_select_fusion
  8.6 0.3 convert_reduce_fusion
  9.0 0.2 select_reduce_fusion
  9.2 0.1 copy.15.mirror_ref
  9.4 0.1 copy.14.place_ref
  9.6 0.8 copy.16.pair_ref
  10.4 0.8 broadcast_add_fusion
  11.2 0.1 add.83.occ_ref
  11.3 27.9 %all-gather.place_ref = s32[8,1,512]{2,1,0:T(1,128)S(1)} all-gather(s32[1,1,512]{2,1,0:T(1,128)S(1)} %bitcast.10), channel_id=1, replica_groups=mesh['row'=4,'col'=8] {'col'}, dimensions={0}, use_global_device_ids=true | all-gather | bytes 18432 | tf_op jit(solution)/shard_map/all_gather | solution.py:229
  39.2 0.8 select_reduce_fusion.1.slot_ref
  40.0 29.1 %sort_rows.1 = (bf16[8,288,2048]{2,1,0:T(8,128)(2,1)}, bf16[8,224,2048]{2,1,0:T(8,128)(2,1)S(1)}, bf16[1024,1024]{1,0:T(8,128)(2,1)S(1)}) custom-call(s32[32]{0:T(128)S(1)} %select_reduce_fusion.1.slot_ref, s32[32]{0:T(128)S(1)} %compare_convert_fusion.live_ref, bf16[1,1,32,512,512]{4,3,2,1,0:T(8,128)(2,1)} %tile_ref.1, s32[8,1,512]{2,1,0:T(1,128)S(1)} %all-gather.place_ref), custom_call_target="tpu_custom_call" | custom-call | flops 8589934592 | bytes 33554432 | tf_op jit(solution)/shard_map/sort_rows/pallas_call | solution.py:236
  69.1 0.0 copy-start
  69.1 1.3 copy-done
  70.4 0.0 copy-start.3
  70.4 2.9 %copy-done.3 = bf16[8,224,2048]{2,1,0:T(8,128)(2,1)} copy-done((bf16[8,224,2048]{2,1,0:T(8,128)(2,1)}, bf16[8,224,2048]{2,1,0:T(8,128)(2,1)S(1)}, u32[]{:S(2)}) %copy-start.3) | copy-done | bytes 7340056
  73.3 0.0 all-gather.3.cloned.1.call-done
  73.3 139.6 %reduce_pairs.1.z_ref = f32[512,1024]{1,0:T(8,128)} custom-call(bf16[8,288,2048]{2,1,0:T(8,128)(2,1)} %get-tuple-element.8.u_hbm, bf16[8,224,2048]{2,1,0:T(8,128)(2,1)} %copy-done.3, bf16[2048,1024]{1,0:T(8,128)(2,1)} %bitcast.8, bf16[1024,1024]{1,0:T(8,128)(2,1)} %copy-done), custom_call_target="tpu_custom_call" | custom-call | tf_op jit(solution)/shard_map/reduce_pairs/pallas_call | solution.py:266
  213.0 0.0 copy-start.1
  213.0 1.6 copy-done.1
  214.6 0.0 copy-start.2
  214.6 1.6 copy-done.2
  216.2 11.2 %finish_rows.1 = f32[512,1024]{1,0:T(8,128)} custom-call(f32[512,1024]{1,0:T(8,128)S(1)} %copy-done.2, bf16[1024,1024]{1,0:T(8,128)(2,1)S(1)} %copy-done.1, s32[512,1]{1,0:T(8,128)S(1)} %copy.14.place_ref, s32[512,1]{1,0:T(8,128)S(1)} %copy.15.mirror_ref, f32[512,1]{1,0:T(8,128)S(1)} %copy.16.pair_ref, f32[1,1024]{1,0:T(1,128)S(1)} %add.83.occ_ref), custom_call_target="tpu_custom_call" | custom-call | tf_op jit(solution)/shard_map/finish_rows/pallas_call | solution.py:294
  (3 shorter events, 0.0 us)
Async XLA Ops:
  6.5 66.8 %all-gather.3.cloned.1.call-start = ((), (), s32[]{:S(2)}) async-start(), calls=%async_computation | async-start | bytes 5242880 | tf_op jit(solution)/shard_map/all_gather | solution.py:230
  69.1 1.3 copy-start
  70.4 2.9 %copy-start.3 = (bf16[8,224,2048]{2,1,0:T(8,128)(2,1)}, bf16[8,224,2048]{2,1,0:T(8,128)(2,1)S(1)}, u32[]{:S(2)}) copy-start(bf16[8,224,2048]{2,1,0:T(8,128)(2,1)S(1)} %get-tuple-element.9.w_hbm) | copy-start | bytes 22020100
  213.0 1.6 copy-start.1
  214.6 1.6 copy-start.2
Sparse Core Ops, SparseCore 0:
  8.9 37.1 all-gather.2

commit v2 on v1

v2 whole, which is shorter than its diff:
```python
import functools

import jax
import jax.numpy as jnp
from jax import lax
from jax.experimental import pallas as pl
from jax.experimental.pallas import tpu as pltpu
from jax.sharding import PartitionSpec as P

MESH = pl.DeviceIdType.MESH
F32, BF16, I32, I16 = jnp.float32, jnp.bfloat16, jnp.int32, jnp.int16
LEVELS = 32767.0


def iota(shape, axis):
    return lax.broadcasted_iota(I32, shape, axis)


def row_places(partner, me, n):
    rows = partner.shape[0]
    half = rows // n // 2
    own = (n + 1) * half
    local = partner % (n * rows)
    block, within = local // rows, local % rows
    index = jnp.arange(rows, dtype=I32)
    key = jnp.where(block < me, within, index)
    before = (block[None, :] == block[:, None]) & (key[None, :] < key[:, None])
    rank = jnp.sum(before.astype(I32), axis=1)
    shift = (block - me + n) % n
    owned = jnp.where(me < block, rank < half, rank >= half)
    step = (shift - 1) * half + rank % half
    place = jnp.where(block == me, rank, jnp.where(owned, 2 * half + step, own + step))
    found = jnp.sum(jnp.where(index[None, :] == within[:, None], place[None, :], 0), axis=1)
    mirror = jnp.where(block == me, rows + found, -1)
    return place, mirror


def gather_kernel(n, mine_ref, all_ref, landed, send_sem, recv_sem):
    me = lax.axis_index("col")
    barrier = pltpu.get_barrier_semaphore()
    for d in range(1, n):
        pl.semaphore_signal(barrier, inc=1, device_id={"col": lax.rem(me + d, n)}, device_id_type=MESH)
    pl.semaphore_wait(barrier, n - 1)

    def copy(d):
        return pltpu.make_async_remote_copy(
            src_ref=mine_ref, dst_ref=landed.at[d], send_sem=send_sem.at[d], recv_sem=recv_sem.at[d],
            device_id={"col": lax.rem(me + d, n)}, device_id_type=MESH,
        )

    for d in range(1, n):
        copy(d).start()
    all_ref[me] = mine_ref[...]
    for d in range(1, n):
        copy(d).wait_recv()
        all_ref[lax.rem(me + n - d, n)] = landed[d]
    for d in range(1, n):
        copy(d).wait_send()


def sort_kernel(n, half, occ, bc, slot_ref, live_ref, *refs):
    tiles, (place_ref, u_ref, w_ref, swap_ref) = refs[:bc], refs[bc:]
    i = pl.program_id(0)
    rows = place_ref.shape[2]
    tile = tiles[0].shape[3]
    own = (n + 1) * half

    total = swap_ref.shape[1]
    chunk = swap_ref.shape[0]
    x = iota((chunk, total), 0) + i * chunk
    y = iota((chunk, total), 1)
    swap_ref[...] = (x == (y % occ) * occ + y // occ).astype(F32).astype(BF16)

    for j in range(tile // rows):
        o = i * (tile // rows) + j
        equal = iota((rows, rows), 0) == place_ref[o]
        for c in range(bc):
            hit = equal & (live_ref[i * bc + c] > 0)
            one_hot = hit.astype(F32).astype(BF16)
            got = jnp.dot(one_hot, tiles[c][0, 0, 0, j * rows : (j + 1) * rows, :], preferred_element_type=F32)
            at = slice(c * tile, (c + 1) * tile)
            u_ref[j, :, at] = got[:own].astype(BF16)
            for d in range(1, n):
                a = lax.rem(o + d, n)
                start = (n - d - 1) * half
                w_ref[a, start : start + half, at] = got[own + (d - 1) * half : own + d * half].astype(BF16)


def reduce_kernel(
    n, half, ranks, u_hbm, w_hbm, swap_hbm, *refs
):
    pieces, refs = refs[:ranks], refs[ranks:]
    (
        z_ref, ubuf, wbuf, tall, t2buf, swap, sbuf, q1s, s1s, q1r, s1r, q2s, s2s, q2r, s2r, xqs, xss, xqr, xsr,
        usem, wsem, tsem, psem, q1a, q1b, s1a, s1b, q2a, q2b, s2a, s2b, xqa, xqb, xsa, xsb,
    ) = refs
    me = lax.axis_index("col")
    row = lax.axis_index("row")
    levels = n // 2
    level, side = me // 2, lax.rem(me, 2)
    other = me + 1 - 2 * side
    bc, tile, width = tall.shape
    depth = bc * tile
    share = tile // ranks
    own = (n + 1) * half
    chunks = n + 1

    def load_t(k):
        source = lax.rem(row + 2 * (k // 2), ranks)
        source = source if k % 2 == 0 else source + 1 - 2 * lax.rem(source, 2)
        first = pl.multiple_of(source * share, share)
        return pltpu.make_async_copy(pieces[k], tall.at[:, pl.ds(first, share), :], tsem.at[k])

    load_p = pltpu.make_async_copy(swap_hbm, swap, psem)
    for k in range(ranks):
        load_t(k).start()
    load_p.start()

    def load(a):
        return (
            pltpu.make_async_copy(u_hbm.at[a], ubuf.at[a], usem.at[a]),
            pltpu.make_async_copy(w_hbm.at[a], wbuf.at[a], wsem.at[a]),
        )

    def owner(k, of_side):
        return 2 * lax.rem(level + 1 + k, levels) + of_side

    for of_side in (1 - side, side):
        for k in range(levels):
            for copy in load(owner(k, of_side)):
                copy.start()

    barrier = pltpu.get_barrier_semaphore()
    for d in range(1, n):
        pl.semaphore_signal(barrier, inc=1, device_id={"col": lax.rem(me + d, n)}, device_id_type=MESH)
    pl.semaphore_wait(barrier, n - 1)

    for k in range(ranks):
        load_t(k).wait()
    load_p.wait()
    high = 256
    per = tile // high

    @pl.loop(0, depth // high)
    def _(k):
        at = pl.ds(pl.multiple_of(k * high, high), high)
        source = tall.at[k // per, pl.ds(pl.multiple_of(lax.rem(k, per) * high, high), high), :]
        for c in range(0, width, 256):
            t2buf[at, c : c + 256] = jnp.dot(source[...], swap[:, c : c + 256], preferred_element_type=F32).astype(BF16)

    def product(a, out):
        for copy in load(a):
            copy.wait()

        @pl.loop(0, width // 256)
        def _(c):
            at = pl.ds(pl.multiple_of(c * 256, 256), 256)
            first = jnp.dot(ubuf[a], tall[:, :, at].reshape(depth, 256), preferred_element_type=F32)
            second = jnp.dot(wbuf[a], t2buf[:, at], preferred_element_type=F32)
            out[0 : 2 * half, at] = first[: 2 * half]
            out[2 * half : own, at] = first[2 * half :] + second

    def remote(source, target, sent, arrived, device):
        return pltpu.make_async_remote_copy(
            src_ref=source, dst_ref=target, send_sem=sent, recv_sem=arrived,
            device_id={"col": device}, device_id_type=MESH,
        )

    def first_copy(k):
        return (
            remote(q1s.at[k], q1r.at[k], q1a.at[k], q1b.at[k], other),
            remote(s1s.at[k], s1r.at[k], s1a.at[k], s1b.at[k], other),
        )

    def second_copy(k):
        device = owner(k, side)
        return (
            remote(q2s.at[k], q2r.at[k], q2a.at[k], q2b.at[k], device),
            remote(s2s.at[k], s2r.at[k], s2a.at[k], s2b.at[k], device),
        )

    diagonal = iota((half, 128), 0) == iota((half, 128), 1)

    def to_levels(part):
        most = jnp.max(jnp.abs(part), axis=1, keepdims=True)
        inverse = jnp.where(most > 1e-30, LEVELS / jnp.maximum(most, 1e-30), 0.0)
        scale = jnp.sum(jnp.where(diagonal, most * (1.0 / LEVELS), 0.0), axis=0, keepdims=True)
        return jnp.round(part * inverse).astype(I32).astype(I16), scale

    def from_levels(value, scale):
        return value.astype(I32).astype(F32) * jnp.sum(jnp.where(diagonal, scale, 0.0), axis=1, keepdims=True)

    @pl.loop(0, levels)
    def _(k):
        product(owner(k, 1 - side), sbuf)
        for m in range(chunks):
            q1s[k, m], s1s[k, m : m + 1, :] = to_levels(sbuf[m * half : (m + 1) * half, :])
        for copy in first_copy(k):
            copy.start()

    @pl.loop(0, levels - 1)
    def _(k):
        product(owner(k, side), sbuf)
        for copy in first_copy(k):
            copy.wait_recv()
        for m in range(chunks):
            part = sbuf[m * half : (m + 1) * half, :] + from_levels(q1r[k, m], s1r[k, m : m + 1, :])
            q2s[k, m], s2s[k, m : m + 1, :] = to_levels(part)
        for copy in second_copy(k):
            copy.start()

    product(me, z_ref)

    def take(k, value, scale):
        for m in range(chunks):
            z_ref[m * half : (m + 1) * half, :] += from_levels(value[k, m], scale[k, m : m + 1, :])

    for copy in first_copy(levels - 1):
        copy.wait_recv()
    take(levels - 1, q1r, s1r)

    @pl.loop(0, levels - 1)
    def _(k):
        for copy in second_copy(k):
            copy.wait_recv()
        take(k, q2r, s2r)

    def last_copy(d):
        device = lax.rem(me + d, n)
        return (
            remote(xqs.at[d], xqr.at[n - d], xqa.at[d], xqb.at[n - d], device),
            remote(xss.at[d], xsr.at[n - d], xsa.at[d], xsb.at[n - d], device),
        )

    for d in range(1, n):
        xqs[d], xss[d, 0:1, :] = to_levels(z_ref[(d + 1) * half : (d + 2) * half, :])
        for copy in last_copy(d):
            copy.start()
    for d in range(1, n):
        for copy in last_copy(d):
            copy.wait_recv()
    for d in range(1, n):
        z_ref[own + (d - 1) * half : own + d * half, :] = from_levels(xqr[d], xsr[d, 0:1, :])
    for d in range(1, n):
        for copy in last_copy(d):
            copy.wait_send()

    @pl.loop(0, levels)
    def _(k):
        for copy in first_copy(k):
            copy.wait_send()

    @pl.loop(0, levels - 1)
    def _(k):
        for copy in second_copy(k):
            copy.wait_send()


def final_kernel(half, own, z_ref, swap_ref, place_ref, mirror_ref, pair_ref, occ_ref, out_ref, pieces):
    rows, width = z_ref.shape

    @pl.when(pl.program_id(0) == 0)
    def _():
        rest = z_ref[...]
        for p in range(2):
            piece = rest.astype(BF16)
            pieces[p] = piece
            rest = rest - piece.astype(F32)

    chunk = out_ref.shape[1]
    at = pl.ds(pl.multiple_of(pl.program_id(0) * chunk, chunk), chunk)
    place, mirror = place_ref[...], mirror_ref[...]

    def hot(count, first):
        number = iota((rows, count), 1) + first
        return ((number == place) | (number == mirror)).astype(F32).astype(BF16)

    hot_own, hot_far, hot_self = hot(own, 0), hot(rows - own, own), hot(2 * half, rows)
    mixer = swap_ref[...]
    total = None
    for p in (1, 0):
        far = jnp.dot(pieces[p, own:, :], mixer, preferred_element_type=F32).astype(BF16)
        near = jnp.dot(pieces[p, : 2 * half, :], mixer, preferred_element_type=F32).astype(BF16)
        term = jnp.dot(hot_own, pieces[p, :own, at], preferred_element_type=F32)
        mine = jnp.dot(hot_self, near, preferred_element_type=F32)
        other = jnp.dot(hot_far, far, preferred_element_type=F32)
        term = term + (mine + other)
        total = term if total is None else total + term
    out_ref[...] = total / (pair_ref[...] - occ_ref[...])


def body(integrals, tile_count, tile_list, amplitudes, pair_energy, occ_energy, partner):
    n = lax.axis_size("col")
    me = lax.axis_index("col")
    rows = partner.shape[0]
    half = rows // n // 2
    own = (n + 1) * half
    slots, tile = integrals.shape[2], integrals.shape[3]
    bc, _, width = amplitudes.shape
    br = slots // bc
    occ = occ_energy.shape[0]
    depth = bc * tile

    place, mirror = row_places(partner, me, n)
    ranks = lax.axis_size("row")
    pieces = [amplitudes]
    for k in range(2, ranks, 2):
        pieces.append(lax.ppermute(amplitudes, "row", [((r + k) % ranks, r) for r in range(ranks)]))
    pieces = [q for p in pieces for q in (p, lax.ppermute(p, "row", [(r ^ 1, r) for r in range(ranks)]))]

    dma = pltpu.SemaphoreType.DMA
    places = pl.pallas_call(
        functools.partial(gather_kernel, n),
        out_shape=jax.ShapeDtypeStruct((n, 1, rows), I32),
        in_specs=[pl.BlockSpec(memory_space=pltpu.VMEM)],
        out_specs=pl.BlockSpec(memory_space=pltpu.VMEM),
        scratch_shapes=[pltpu.VMEM((n, 1, rows), I32), dma((n,)), dma((n,))],
        compiler_params=pltpu.CompilerParams(collective_id=1, has_side_effects=True),
        name="gather_places",
    )(place[None, :])

    number = jnp.arange(slots, dtype=I32)
    slot = jnp.sum(jnp.where(tile_list[0, 0][None, :] == number[:, None], number[None, :], 0), axis=1)
    live = (slot < tile_count[0, 0]).astype(I32)

    per = tile // rows

    def tile_spec(c):
        return pl.BlockSpec((1, 1, 1, tile, tile), lambda i, s, l: (0, 0, s[i * bc + c], 0, 0))

    u, w, swap = pl.pallas_call(
        functools.partial(sort_kernel, n, half, occ, bc),
        grid_spec=pltpu.PrefetchScalarGridSpec(
            num_scalar_prefetch=2,
            grid=(br,),
            in_specs=[tile_spec(c) for c in range(bc)] + [pl.BlockSpec((n, 1, rows), lambda i, s, l: (0, 0, 0))],
            out_specs=[
                pl.BlockSpec((per, own, depth), lambda i, s, l: (i, 0, 0)),
                pl.BlockSpec((n, rows - own, depth), lambda i, s, l: (0, 0, 0)),
                pl.BlockSpec((width // br, width), lambda i, s, l: (i, 0)),
            ],
        ),
        out_shape=[
            jax.ShapeDtypeStruct((n, own, depth), BF16),
            jax.ShapeDtypeStruct((n, rows - own, depth), BF16),
            jax.ShapeDtypeStruct((width, width), BF16),
        ],
        compiler_params=pltpu.CompilerParams(vmem_limit_bytes=48 * 1024 * 1024),
        cost_estimate=pl.CostEstimate(
            flops=2 * slots * rows * tile * tile, bytes_accessed=4 * slots * tile * tile, transcendentals=0
        ),
        name="sort_rows",
    )(slot, live, *([integrals] * bc), places)

    anywhere = pl.BlockSpec(memory_space=pl.ANY)
    scale_rows = -(-(n + 1) // 8) * 8
    levels = n // 2
    packed = [pltpu.VMEM((levels, n + 1, half, width), I16), pltpu.VMEM((levels, scale_rows, 128), F32)]
    last = [pltpu.VMEM((n, half, width), I16), pltpu.VMEM((n, 8, 128), F32)]
    z = pl.pallas_call(
        functools.partial(reduce_kernel, n, half, ranks),
        out_shape=jax.ShapeDtypeStruct((rows, width), F32),
        in_specs=[anywhere] * (3 + ranks),
        out_specs=pl.BlockSpec(memory_space=pltpu.VMEM),
        scratch_shapes=[
            pltpu.VMEM((n, own, depth), BF16),
            pltpu.VMEM((n, rows - own, depth), BF16),
            pltpu.VMEM((bc, tile, width), BF16),
            pltpu.VMEM((depth, width), BF16),
            pltpu.VMEM((width, width), BF16),
            pltpu.VMEM((own, width), F32),
            *(packed * 4),
            *(last * 2),
            dma((n,)), dma((n,)), dma((ranks,)), dma,
            *([dma((levels,))] * 8),
            *([dma((n,))] * 4),
        ],
        compiler_params=pltpu.CompilerParams(
            collective_id=0, has_side_effects=True, vmem_limit_bytes=63 * 1024 * 1024
        ),
        name="reduce_pairs",
    )(u, w, swap, *pieces)

    chunk = 256
    whole = lambda k: (0, 0)
    return pl.pallas_call(
        functools.partial(final_kernel, half, own),
        grid=(width // chunk,),
        in_specs=[
            pl.BlockSpec((rows, width), whole),
            pl.BlockSpec((width, chunk), lambda k: (0, k)),
            pl.BlockSpec((rows, 1), whole),
            pl.BlockSpec((rows, 1), whole),
            pl.BlockSpec((rows, 1), whole),
            pl.BlockSpec((1, chunk), lambda k: (0, k)),
        ],
        out_specs=pl.BlockSpec((rows, chunk), lambda k: (0, k)),
        out_shape=jax.ShapeDtypeStruct((rows, width), F32),
        scratch_shapes=[pltpu.VMEM((2, rows, width), BF16)],
        compiler_params=pltpu.CompilerParams(vmem_limit_bytes=40 * 1024 * 1024),
        name="finish_rows",
    )(
        z, swap, place[:, None], mirror[:, None], pair_energy[:, None],
        (occ_energy[:, None] + occ_energy[None, :]).reshape(1, width),
    )


def solution(mesh):
    return jax.shard_map(
        body,
        mesh=mesh,
        in_specs=(
            P("row", "col", None, None, None),
            P("row", "col"),
            P("row", "col", None),
            P("col", "row", None),
            P(("row", "col")),
            P(),
            P(("row", "col")),
        ),
        out_specs=P(("row", "col"), None),
        check_vma=False,
    )
```

time: 238 us -> 168 us (0.71)
  the two profiles are of different devices: /device:TPU:0 before, /device:TPU:26 now
where the time goes in v2:
time: 168 us
  Pallas kernels  133 us (79%)
  waiting for transfers between devices  21.4 us (13%)
  local copies, waits for them, and re-layouts  8.06 us (5%)
  other arithmetic  2.91 us (2%)
    pallas_call x1, Pallas kernels, body(): pl.pallas_call(functools.partial(reduce_kernel, n, half, ranks), out_shap...  99.1 us
    ppermute x1, waiting for transfers between devices, body(): lax.ppermute(amplitudes, 'row', [((r + k) % ranks, r) for r in range(rank...  21.4 us
    pallas_call x1, Pallas kernels, body(): pl.pallas_call(functools.partial(sort_kernel, n, half, occ, bc), grid_spe...  17.7 us
    pallas_call x1, Pallas kernels, body(): pl.pallas_call(functools.partial(final_kernel, half, own), grid=(width //...  8.35 us
    pallas_call x1, Pallas kernels, body(): pl.pallas_call(functools.partial(gather_kernel, n), out_shape=jax.ShapeDt...  7.84 us
    unnamed x14, local copies, waits for them, and re-layouts  6.19 us
  transfers between devices with their start and end apart: 3, of which 1 were waited for; matrix products, arithmetic and copies ran while one was open for 3% of the time, Pallas kernels for 15%

profile of v2, /device:TPU:26, one launch (start us, length us, event | category | flops | bytes accessed | tf_op | source)
XLA Modules:
  0.0 167.6 jit_solution(255809819287228070)
XLA Ops:
  0.0 1.5 collective-permute-start.1
  1.5 0.7 iota_select_fusion
  2.2 0.3 convert_reduce_fusion
  2.6 0.0 copy-start.6
  2.6 0.2 select_reduce_fusion
  2.9 0.8 broadcast_add_fusion
  3.7 21.4 %collective-permute-done.1.refs_2_ = bf16[4,128,1024]{2,1,0:T(8,128)(2,1)S(1)} collective-permute-done((bf16[4,128,1024]{2,1,0:T(8,128)(2,1)}, bf16[4,128,1024]{2,1,0:T(8,128)(2,1)S(1)}, u32[]{:S(2)}, u32[]{:S(2)}) %collective-permute-start.1) | collective-permute-done | bytes 1048608 | tf_op jit(solution)/shard_map/ppermute | solution.py:308
  25.1 0.8 select_reduce_fusion.1.slot_ref
  25.9 7.8 %gather_places.1.refs_4_ = s32[8,1,512]{2,1,0:T(1,128)} custom-call(s32[1,512]{1,0:T(1,128)} %bitcast.7), custom_call_target="tpu_custom_call" | custom-call | tf_op jit(solution)/shard_map/gather_places/pallas_call | solution.py:312
  34.4 0.1 copy.12.mirror_ref
  34.6 0.8 copy.11.place_ref
  35.4 0.8 copy.13.pair_ref
  36.2 0.1 add.83.occ_ref
  36.3 0.7 copy-done.3
  37.0 17.7 %sort_rows.1 = (bf16[8,288,2048]{2,1,0:T(8,128)(2,1)}, bf16[8,224,2048]{2,1,0:T(8,128)(2,1)}, bf16[1024,1024]{1,0:T(8,128)(2,1)S(1)}) custom-call(s32[32]{0:T(128)S(1)} %select_reduce_fusion.1.slot_ref, s32[32]{0:T(128)S(1)} %compare_convert_fusion.live_ref, bf16[1,1,32,512,512]{4,3,2,1,0:T(8,128)(2,1)} %refs_3_.1, bf16[1,1,32,512,512]{4,3,2,1,0:T(8,128)(2,1)} %refs_3_.1, ...), custom_call_target="tpu_custom_call" | custom-call | flops 8589934592 | bytes 33554432 | tf_op jit(solution)/shard_map/sort_rows/pallas_call | solution.py:331
  54.7 0.0 copy-start
  54.7 1.3 copy-done
  56.0 0.0 collective-permute-done.refs_1_
  56.0 1.0 copy-done.5
  57.0 99.1 %reduce_pairs.1.z_ref = f32[512,1024]{1,0:T(8,128)} custom-call(bf16[8,288,2048]{2,1,0:T(8,128)(2,1)} %get-tuple-element.8.u_hbm, bf16[8,224,2048]{2,1,0:T(8,128)(2,1)} %get-tuple-element.9.w_hbm, bf16[1024,1024]{1,0:T(8,128)(2,1)} %copy-done, bf16[4,128,1024]{2,1,0:T(8,128)(2,1)} %refs_0_.3, bf16[4,128,1024]{2,1,0:T(8,128)(2,1)} %copy-done.5, ...), custom_call_target="tpu_custom_call" | custom-call | tf_op jit(solution)/shard_map/reduce_pairs/pallas_call | solution.py:360
  156.1 0.0 copy-start.1
  156.1 1.6 copy-done.1
  157.7 1.6 copy-done.2
  159.3 8.3 %finish_rows.1 = f32[512,1024]{1,0:T(8,128)} custom-call(f32[512,1024]{1,0:T(8,128)S(1)} %copy-done.2, bf16[1024,1024]{1,0:T(8,128)(2,1)S(1)} %copy-done.1, s32[512,1]{1,0:T(8,128)S(1)} %copy.11.place_ref, s32[512,1]{1,0:T(8,128)S(1)} %copy.12.mirror_ref, f32[512,1]{1,0:T(8,128)S(1)} %copy.13.pair_ref, f32[1,1024]{1,0:T(1,128)S(1)} %add.83.occ_ref), custom_call_target="tpu_custom_call" | custom-call | tf_op jit(solution)/shard_map/finish_rows/pallas_call | solution.py:386
  (12 shorter events, 0.0 us)
Async XLA Ops:
  0.0 25.1 %collective-permute-start.1 = (bf16[4,128,1024]{2,1,0:T(8,128)(2,1)}, bf16[4,128,1024]{2,1,0:T(8,128)(2,1)S(1)}, u32[]{:S(2)}, u32[]{:S(2)}) collective-permute-start(bf16[4,128,1024]{2,1,0:T(8,128)(2,1)} %refs_0_.3), channel_id=1, source_target_pairs={{16,0},{24,8},{0,16},{8,24},{17,1},{25,9},{1,17},{9,25},{18,2},{26... | collective-permute-start | bytes 3145736 | tf_op jit(solution)/shard_map/ppermute | solution.py:308
  1.5 54.5 %collective-permute-start = (bf16[4,128,1024]{2,1,0:T(8,128)(2,1)}, bf16[4,128,1024]{2,1,0:T(8,128)(2,1)S(1)}, u32[]{:S(2)}, u32[]{:S(2)}) collective-permute-start(bf16[4,128,1024]{2,1,0:T(8,128)(2,1)} %refs_0_.3), channel_id=1, source_target_pairs={{8,0},{0,8},{24,16},{16,24},{9,1},{1,9},{25,17},{17,25},{10,2},{2,... | collective-permute-start | bytes 3145736 | tf_op jit(solution)/shard_map/ppermute | solution.py:309
  2.6 23.3 %copy-start.6 = (s32[512]{0:T(512)}, s32[512]{0:T(512)S(1)}, u32[]{:S(2)}) copy-start(s32[512]{0:T(512)S(1)} %select_select_fusion) | copy-start | bytes 6148
  25.1 29.6 %copy-start.4 = (bf16[4,128,1024]{2,1,0:T(8,128)(2,1)}, bf16[4,128,1024]{2,1,0:T(8,128)(2,1)S(1)}, u32[]{:S(2)}) copy-start(bf16[4,128,1024]{2,1,0:T(8,128)(2,1)S(1)} %collective-permute-done.1.refs_2_) | copy-start | bytes 3145732
  25.1 30.9 %collective-permute-start.2 = (bf16[4,128,1024]{2,1,0:T(8,128)(2,1)S(1)}, bf16[4,128,1024]{2,1,0:T(8,128)(2,1)}, u32[]{:S(2)}, u32[]{:S(2)}) collective-permute-start(bf16[4,128,1024]{2,1,0:T(8,128)(2,1)S(1)} %collective-permute-done.1.refs_2_), channel_id=1, source_target_pairs={{8,0},{0,8},{24,16},{16,24},{9,1},{1,9},{25,17},{17,25},{10,2},{2,... | collective-permute-start | bytes 3145736 | tf_op jit(solution)/shard_map/ppermute | solution.py:309
  36.3 0.7 copy-start.3
  54.7 1.3 copy-start
  56.0 1.0 copy-start.5
  156.1 1.6 copy-start.1
  157.7 1.6 copy-start.2

commit v3 on v2

--- a/solution.py
+++ b/solution.py
@@ -87,12 +87,16 @@
 
 
 def reduce_kernel(
-    n, half, ranks, u_hbm, w_hbm, swap_hbm, *refs
+    n, half, ranks, wide, u_hbm, w_hbm, swap_hbm, *refs
 ):
-    pieces, refs = refs[:ranks], refs[ranks:]
+    held = ranks // 2 + 1
+    given, refs = refs[:held], refs[held:]
+    pieces = [given[0], given[1]]
+    for piece in given[2:]:
+        pieces += [piece, None]
     (
         z_ref, ubuf, wbuf, tall, t2buf, swap, sbuf, q1s, s1s, q1r, s1r, q2s, s2s, q2r, s2r, xqs, xss, xqr, xsr,
-        usem, wsem, tsem, psem, q1a, q1b, s1a, s1b, q2a, q2b, s2a, s2b, xqa, xqb, xsa, xsb,
+        usem, wsem, tsem, psem, q1a, q1b, s1a, s1b, q2a, q2b, s2a, s2b, xqa, xqb, xsa, xsb, psend, precv,
     ) = refs
     me = lax.axis_index("col")
     row = lax.axis_index("row")
@@ -111,8 +115,17 @@
         first = pl.multiple_of(source * share, share)
         return pltpu.make_async_copy(pieces[k], tall.at[:, pl.ds(first, share), :], tsem.at[k])
 
+    def swap_t(k):
+        first = pl.multiple_of(lax.rem(row + 2 * (k // 2), ranks) * share, share)
+        return pltpu.make_async_remote_copy(
+            src_ref=pieces[k], dst_ref=tall.at[:, pl.ds(first, share), :], send_sem=psend.at[k], recv_sem=precv.at[k],
+            device_id={"row": row + 1 - 2 * lax.rem(row, 2)}, device_id_type=MESH,
+        )
+
+    local = [k for k in range(ranks) if pieces[k] is not None]
+    crossed = [k - 1 for k in range(ranks) if pieces[k] is None]
     load_p = pltpu.make_async_copy(swap_hbm, swap, psem)
-    for k in range(ranks):
+    for k in local:
         load_t(k).start()
     load_p.start()
 
@@ -133,32 +146,29 @@
     barrier = pltpu.get_barrier_semaphore()
     for d in range(1, n):
         pl.semaphore_signal(barrier, inc=1, device_id={"col": lax.rem(me + d, n)}, device_id_type=MESH)
-    pl.semaphore_wait(barrier, n - 1)
-
-    for k in range(ranks):
+    pl.semaphore_signal(barrier, inc=1, device_id={"row": row + 1 - 2 * lax.rem(row, 2)}, device_id_type=MESH)
+    pl.semaphore_wait(barrier, n)
+
+    for k in crossed:
+        swap_t(k).start()
+    for k in local:
         load_t(k).wait()
     load_p.wait()
+    for k in crossed:
+        swap_t(k).wait_recv()
     high = 256
     per = tile // high
-
-    @pl.loop(0, depth // high)
-    def _(k):
-        at = pl.ds(pl.multiple_of(k * high, high), high)
-        source = tall.at[k // per, pl.ds(pl.multiple_of(lax.rem(k, per) * high, high), high), :]
-        for c in range(0, width, 256):
-            t2buf[at, c : c + 256] = jnp.dot(source[...], swap[:, c : c + 256], preferred_element_type=F32).astype(BF16)
-
-    def product(a, out):
-        for copy in load(a):
-            copy.wait()
-
-        @pl.loop(0, width // 256)
-        def _(c):
-            at = pl.ds(pl.multiple_of(c * 256, 256), 256)
-            first = jnp.dot(ubuf[a], tall[:, :, at].reshape(depth, 256), preferred_element_type=F32)
-            second = jnp.dot(wbuf[a], t2buf[:, at], preferred_element_type=F32)
-            out[0 : 2 * half, at] = first[: 2 * half]
-            out[2 * half : own, at] = first[2 * half :] + second
+    parts = width // wide
+
+    def columns(c):
+        return pl.ds(pl.multiple_of(c * wide, wide), wide)
+
+    def product(a, c, out, out_at):
+        at = columns(c)
+        first = jnp.dot(ubuf[a], tall[:, :, at].reshape(depth, wide), preferred_element_type=F32)
+        second = jnp.dot(wbuf[a], t2buf[:, at], preferred_element_type=F32)
+        out[0 : 2 * half, out_at] = first[: 2 * half]
+        out[2 * half : own, out_at] = first[2 * half :] + second
 
     def remote(source, target, sent, arrived, device):
         return pltpu.make_async_remote_copy(
@@ -166,94 +176,158 @@
             device_id={"col": device}, device_id_type=MESH,
         )
 
-    def first_copy(k):
+    def first_copy(c, k):
+        u = c * levels + k
         return (
-            remote(q1s.at[k], q1r.at[k], q1a.at[k], q1b.at[k], other),
-            remote(s1s.at[k], s1r.at[k], s1a.at[k], s1b.at[k], other),
-        )
-
-    def second_copy(k):
+            remote(q1s.at[u], q1r.at[u], q1a.at[u], q1b.at[u], other),
+            remote(s1s.at[u], s1r.at[u], s1a.at[u], s1b.at[u], other),
+        )
+
+    def second_copy(c, k):
         device = owner(k, side)
+        u = c * levels + k
         return (
-            remote(q2s.at[k], q2r.at[k], q2a.at[k], q2b.at[k], device),
-            remote(s2s.at[k], s2r.at[k], s2a.at[k], s2b.at[k], device),
-        )
-
-    diagonal = iota((half, 128), 0) == iota((half, 128), 1)
-
-    def to_levels(part):
+            remote(q2s.at[u], q2r.at[u], q2a.at[u], q2b.at[u], device),
+            remote(s2s.at[u], s2r.at[u], s2a.at[u], s2b.at[u], device),
+        )
+
+    def last_copy(c, d):
+        device = lax.rem(me + d, n)
+        u, v = c * n + d, c * n + n - d
+        return (
+            remote(xqs.at[u], xqr.at[v], xqa.at[u], xqb.at[v], device),
+            remote(xss.at[u], xsr.at[v], xsa.at[u], xsb.at[v], device),
+        )
+
+    group = 128 // half
+    lane, line = iota((half, 128), 1), iota((half, 128), 0)
+
+    def to_levels(part, m):
         most = jnp.max(jnp.abs(part), axis=1, keepdims=True)
         inverse = jnp.where(most > 1e-30, LEVELS / jnp.maximum(most, 1e-30), 0.0)
-        scale = jnp.sum(jnp.where(diagonal, most * (1.0 / LEVELS), 0.0), axis=0, keepdims=True)
+        here = lane == line + (m % group) * half
+        scale = jnp.sum(jnp.where(here, most * (1.0 / LEVELS), 0.0), axis=0, keepdims=True)
         return jnp.round(part * inverse).astype(I32).astype(I16), scale
 
-    def from_levels(value, scale):
-        return value.astype(I32).astype(F32) * jnp.sum(jnp.where(diagonal, scale, 0.0), axis=1, keepdims=True)
-
-    @pl.loop(0, levels)
-    def _(k):
-        product(owner(k, 1 - side), sbuf)
-        for m in range(chunks):
-            q1s[k, m], s1s[k, m : m + 1, :] = to_levels(sbuf[m * half : (m + 1) * half, :])
-        for copy in first_copy(k):
-            copy.start()
-
-    @pl.loop(0, levels - 1)
-    def _(k):
-        product(owner(k, side), sbuf)
-        for copy in first_copy(k):
-            copy.wait_recv()
-        for m in range(chunks):
-            part = sbuf[m * half : (m + 1) * half, :] + from_levels(q1r[k, m], s1r[k, m : m + 1, :])
-            q2s[k, m], s2s[k, m : m + 1, :] = to_levels(part)
-        for copy in second_copy(k):
-            copy.start()
-
-    product(me, z_ref)
-
-    def take(k, value, scale):
-        for m in range(chunks):
-            z_ref[m * half : (m + 1) * half, :] += from_levels(value[k, m], scale[k, m : m + 1, :])
-
-    for copy in first_copy(levels - 1):
-        copy.wait_recv()
-    take(levels - 1, q1r, s1r)
-
-    @pl.loop(0, levels - 1)
-    def _(k):
-        for copy in second_copy(k):
-            copy.wait_recv()
-        take(k, q2r, s2r)
-
-    def last_copy(d):
-        device = lax.rem(me + d, n)
-        return (
-            remote(xqs.at[d], xqr.at[n - d], xqa.at[d], xqb.at[n - d], device),
-            remote(xss.at[d], xsr.at[n - d], xsa.at[d], xsb.at[n - d], device),
-        )
-
-    for d in range(1, n):
-        xqs[d], xss[d, 0:1, :] = to_levels(z_ref[(d + 1) * half : (d + 2) * half, :])
-        for copy in last_copy(d):
-            copy.start()
-    for d in range(1, n):
-        for copy in last_copy(d):
-            copy.wait_recv()
-    for d in range(1, n):
-        z_ref[own + (d - 1) * half : own + d * half, :] = from_levels(xqr[d], xsr[d, 0:1, :])
-    for d in range(1, n):
-        for copy in last_copy(d):
-            copy.wait_send()
-
-    @pl.loop(0, levels)
-    def _(k):
-        for copy in first_copy(k):
-            copy.wait_send()
-
-    @pl.loop(0, levels - 1)
-    def _(k):
-        for copy in second_copy(k):
-            copy.wait_send()
+    def from_levels(value, scale, m):
+        here = lane == line + (m % group) * half
+        return value.astype(I32).astype(F32) * jnp.sum(jnp.where(here, scale, 0.0), axis=1, keepdims=True)
+
+    def pack(u, value, q, s):
+        for g in range(0, chunks, group):
+            line_of = None
+            for m in range(g, min(g + group, chunks)):
+                q[u, m], scale = to_levels(value(m), m)
+                line_of = scale if line_of is None else line_of + scale
+            s[u, g // group : g // group + 1, :] = line_of
+
+    def unpack(u, m, q, s):
+        return from_levels(q[u, m], s[u, m // group : m // group + 1, :], m)
+
+    def rows_of(m):
+        return slice(m * half, (m + 1) * half)
+
+    @pl.loop(0, parts + 2)
+    def _(turn):
+        @pl.when(turn < parts)
+        def _():
+            at = columns(turn)
+
+            @pl.loop(0, depth // high)
+            def _(k):
+                source = tall.at[k // per, pl.ds(pl.multiple_of(lax.rem(k, per) * high, high), high), :]
+                t2buf[pl.ds(pl.multiple_of(k * high, high), high), at] = jnp.dot(
+                    source[...], swap[:, at], preferred_element_type=F32
+                ).astype(BF16)
+
+            @pl.loop(0, levels)
+            def _(k):
+                @pl.when(turn == 0)
+                def _():
+                    for copy in load(owner(k, 1 - side)):
+                        copy.wait()
+
+                product(owner(k, 1 - side), turn, sbuf, slice(None))
+                pack(turn * levels + k, lambda m: sbuf[rows_of(m), :], q1s, s1s)
+                for copy in first_copy(turn, k):
+                    copy.start()
+
+        @pl.when((turn >= 1) & (turn <= parts))
+        def _():
+            c = turn - 1
+
+            @pl.loop(0, levels - 1)
+            def _(k):
+                @pl.when(c == 0)
+                def _():
+                    for copy in load(owner(k, side)):
+                        copy.wait()
+
+                product(owner(k, side), c, sbuf, slice(None))
+                for copy in first_copy(c, k):
+                    copy.wait_recv()
+                u = c * levels + k
+                pack(u, lambda m: sbuf[rows_of(m), :] + unpack(u, m, q1r, s1r), q2s, s2s)
+                for copy in second_copy(c, k):
+                    copy.start()
+
+        @pl.when(turn >= 2)
+        def _():
+            c = turn - 2
+
+            @pl.when(c == 0)
+            def _():
+                for copy in load(me):
+                    copy.wait()
+
+            at = columns(c)
+            product(me, c, z_ref, at)
+
+            def take(k, q, s):
+                for m in range(chunks):
+                    z_ref[rows_of(m), at] += unpack(c * levels + k, m, q, s)
+
+            for copy in first_copy(c, levels - 1):
+                copy.wait_recv()
+            take(levels - 1, q1r, s1r)
+
+            @pl.loop(0, levels - 1)
+            def _(k):
+                for copy in second_copy(c, k):
+                    copy.wait_recv()
+                take(k, q2r, s2r)
+
+            for d in range(1, n):
+                xqs[c * n + d], xss[c * n + d] = to_levels(z_ref[rows_of(d + 1), at], 0)
+                for copy in last_copy(c, d):
+                    copy.start()
+
+    @pl.loop(0, parts)
+    def _(c):
+        for d in range(1, n):
+            for copy in last_copy(c, d):
+                copy.wait_recv()
+            v = n - d
+            z_ref[own + (v - 1) * half : own + v * half, columns(c)] = from_levels(xqr[c * n + v], xsr[c * n + v], 0)
+
+    for k in crossed:
+        swap_t(k).wait_send()
+
+    @pl.loop(0, parts)
+    def _(c):
+        for d in range(1, n):
+            for copy in last_copy(c, d):
+                copy.wait_send()
+
+        @pl.loop(0, levels)
+        def _(k):
+            for copy in first_copy(c, k):
+                copy.wait_send()
+
+        @pl.loop(0, levels - 1)
+        def _(k):
+            for copy in second_copy(c, k):
+                copy.wait_send()
 
 
 def final_kernel(half, own, z_ref, swap_ref, place_ref, mirror_ref, pair_ref, occ_ref, out_ref, pieces):
@@ -303,10 +377,9 @@
 
     place, mirror = row_places(partner, me, n)
     ranks = lax.axis_size("row")
-    pieces = [amplitudes]
+    pieces = [amplitudes, lax.ppermute(amplitudes, "row", [(r ^ 1, r) for r in range(ranks)])]
     for k in range(2, ranks, 2):
         pieces.append(lax.ppermute(amplitudes, "row", [((r + k) % ranks, r) for r in range(ranks)]))
-    pieces = [q for p in pieces for q in (p, lax.ppermute(p, "row", [(r ^ 1, r) for r in range(ranks)]))]
 
     dma = pltpu.SemaphoreType.DMA
     places = pl.pallas_call(
@@ -345,7 +418,7 @@
             jax.ShapeDtypeStruct((n, rows - own, depth), BF16),
             jax.ShapeDtypeStruct((width, width), BF16),
         ],
-        compiler_params=pltpu.CompilerParams(vmem_limit_bytes=48 * 1024 * 1024),
+        compiler_params=pltpu.CompilerParams(vmem_limit_bytes=63 * 1024 * 1024),
         cost_estimate=pl.CostEstimate(
             flops=2 * slots * rows * tile * tile, bytes_accessed=4 * slots * tile * tile, transcendentals=0
         ),
@@ -353,14 +426,16 @@
     )(slot, live, *([integrals] * bc), places)
 
     anywhere = pl.BlockSpec(memory_space=pl.ANY)
-    scale_rows = -(-(n + 1) // 8) * 8
-    levels = n // 2
-    packed = [pltpu.VMEM((levels, n + 1, half, width), I16), pltpu.VMEM((levels, scale_rows, 128), F32)]
-    last = [pltpu.VMEM((n, half, width), I16), pltpu.VMEM((n, 8, 128), F32)]
+    wide = 256
+    parts = width // wide
+    scale_rows = -(-(n + 1) // (128 // half))
+    units = parts * (n // 2)
+    packed = [pltpu.VMEM((units, n + 1, half, wide), I16), pltpu.VMEM((units, scale_rows, 128), F32)]
+    last = [pltpu.VMEM((parts * n, half, wide), I16), pltpu.VMEM((parts * n, 1, 128), F32)]
     z = pl.pallas_call(
-        functools.partial(reduce_kernel, n, half, ranks),
+        functools.partial(reduce_kernel, n, half, ranks, wide),
         out_shape=jax.ShapeDtypeStruct((rows, width), F32),
-        in_specs=[anywhere] * (3 + ranks),
+        in_specs=[anywhere] * (3 + len(pieces)),
         out_specs=pl.BlockSpec(memory_space=pltpu.VMEM),
         scratch_shapes=[
             pltpu.VMEM((n, own, depth), BF16),
@@ -368,12 +443,13 @@
             pltpu.VMEM((bc, tile, width), BF16),
             pltpu.VMEM((depth, width), BF16),
             pltpu.VMEM((width, width), BF16),
-            pltpu.VMEM((own, width), F32),
+            pltpu.VMEM((own, wide), F32),
             *(packed * 4),
             *(last * 2),
             dma((n,)), dma((n,)), dma((ranks,)), dma,
-            *([dma((levels,))] * 8),
-            *([dma((n,))] * 4),
+            *([dma((units,))] * 8),
+            *([dma((parts * n,))] * 4),
+            dma((ranks,)), dma((ranks,)),
         ],
         compiler_params=pltpu.CompilerParams(
             collective_id=0, has_side_effects=True, vmem_limit_bytes=63 * 1024 * 1024
@@ -397,7 +473,7 @@
         out_specs=pl.BlockSpec((rows, chunk), lambda k: (0, k)),
         out_shape=jax.ShapeDtypeStruct((rows, width), F32),
         scratch_shapes=[pltpu.VMEM((2, rows, width), BF16)],
-        compiler_params=pltpu.CompilerParams(vmem_limit_bytes=40 * 1024 * 1024),
+        compiler_params=pltpu.CompilerParams(vmem_limit_bytes=63 * 1024 * 1024),
         name="finish_rows",
     )(
         z, swap, place[:, None], mirror[:, None], pair_energy[:, None],

time: 168 us -> 139 us (0.83)
  the two profiles are of different devices: /device:TPU:26 before, /device:TPU:0 now
where the time goes in v3:
time: 139 us
  Pallas kernels  127 us (91%)
  local copies, waits for them, and re-layouts  4.61 us (3%)
  other arithmetic  3.4 us (2%)
  starting transfers between devices  3 us (2%)
    pallas_call x1, Pallas kernels, body(): pl.pallas_call(functools.partial(reduce_kernel, n, half, ranks, wide), ou...  90.8 us
    pallas_call x1, Pallas kernels, body(): pl.pallas_call(functools.partial(sort_kernel, n, half, occ, bc), grid_spe...  18.1 us
    pallas_call x1, Pallas kernels, body(): pl.pallas_call(functools.partial(final_kernel, half, own), grid=(width //...  10 us
    pallas_call x1, Pallas kernels, body(): pl.pallas_call(functools.partial(gather_kernel, n), out_shape=jax.ShapeDt...  8.2 us
  transfers between devices with their start and end apart: 2, of which 0 were waited for; matrix products, arithmetic and copies ran while one was open for 6% of the time, Pallas kernels for 19%

profile of v3, /device:TPU:0, one launch (start us, length us, event | category | flops | bytes accessed | tf_op | source)
XLA Modules:
  0.0 138.9 jit_solution(5532990617427414854)
XLA Ops:
  0.0 0.5 collective-permute-start
  0.5 2.5 %collective-permute-start.1 = (bf16[4,128,1024]{2,1,0:T(8,128)(2,1)}, bf16[4,128,1024]{2,1,0:T(8,128)(2,1)}, u32[]{:S(2)}, u32[]{:S(2)}) collective-permute-start(bf16[4,128,1024]{2,1,0:T(8,128)(2,1)} %refs_0_.3), channel_id=1, source_target_pairs={{16,0},{24,8},{0,16},{8,24},{17,1},{25,9},{1,17},{9,25},{18,2},{26... | collective-permute-start | bytes 3145736 | tf_op jit(solution)/shard_map/ppermute | solution.py:382
  3.0 0.7 iota_select_fusion
  3.7 0.3 convert_reduce_fusion
  4.1 0.0 copy-start
  4.1 0.2 select_reduce_fusion
  4.3 0.8 broadcast_add_fusion
  5.1 0.8 select_reduce_fusion.1.slot_ref
  5.9 0.0 copy-start.1
  5.9 0.0 copy-done
  5.9 8.2 %gather_places.1.refs_4_ = s32[8,1,512]{2,1,0:T(1,128)} custom-call(s32[1,512]{1,0:T(1,128)} %bitcast.7), custom_call_target="tpu_custom_call" | custom-call | tf_op jit(solution)/shard_map/gather_places/pallas_call | solution.py:385
  14.8 0.9 copy.12.mirror_ref
  15.6 1.5 %copy.11.place_ref = s32[512,1]{1,0:T(8,128)} copy(s32[512,1]{0,1:T(1,128)} %bitcast.8) | data formatting | bytes 4096 | tf_op jit(solution)/shard_map/broadcast_in_dim | solution.py:479
  17.2 1.5 %copy.13.pair_ref = f32[512,1]{1,0:T(8,128)} copy(f32[512,1]{0,1:T(1,128)} %bitcast.10) | data formatting | bytes 4096 | tf_op jit(solution)/shard_map/broadcast_in_dim | solution.py:479
  18.7 0.7 add.83.occ_ref
  19.4 0.5 compare_convert_fusion.live_ref
  19.9 0.0 copy-done.1
  19.9 18.1 %sort_rows.1 = (bf16[8,288,2048]{2,1,0:T(8,128)(2,1)}, bf16[8,224,2048]{2,1,0:T(8,128)(2,1)}, bf16[1024,1024]{1,0:T(8,128)(2,1)}) custom-call(s32[32]{0:T(128)} %copy-done.1, s32[32]{0:T(128)} %compare_convert_fusion.live_ref, bf16[1,1,32,512,512]{4,3,2,1,0:T(8,128)(2,1)} %refs_3_.1, bf16[1,1,32,512,512]{4,3,2,1,0:T(8,128)(2,1)} %refs_3_.1, ...), custom_call_target="tpu_custom_call" | custom-call | flops 8589934592 | bytes 33554432 | tf_op jit(solution)/shard_map/sort_rows/pallas_call | solution.py:404
  38.0 0.0 collective-permute-done.refs_1_
  38.0 0.0 collective-permute-done.1.refs_2_
  38.0 90.8 %reduce_pairs.1.z_ref = f32[512,1024]{1,0:T(8,128)} custom-call(bf16[8,288,2048]{2,1,0:T(8,128)(2,1)} %get-tuple-element.8.u_hbm, bf16[8,224,2048]{2,1,0:T(8,128)(2,1)} %get-tuple-element.9.w_hbm, bf16[1024,1024]{1,0:T(8,128)(2,1)} %get-tuple-element.10.swap_hbm.swap_ref, bf16[4,128,1024]{2,1,0:T(8,128)(2,1)} %refs_0_.3, ...), custom_call_target="tpu_custom_call" | custom-call | tf_op jit(solution)/shard_map/reduce_pairs/pallas_call | solution.py:435
  128.8 10.0 %finish_rows.1 = f32[512,1024]{1,0:T(8,128)} custom-call(f32[512,1024]{1,0:T(8,128)} %reduce_pairs.1.z_ref, bf16[1024,1024]{1,0:T(8,128)(2,1)} %get-tuple-element.10.swap_hbm.swap_ref, s32[512,1]{1,0:T(8,128)} %copy.11.place_ref, s32[512,1]{1,0:T(8,128)} %copy.12.mirror_ref, f32[512,1]{1,0:T(8,128)} %copy.13.pair_ref, f32[1,1024]{1,0:T(1,128)} %add.83.occ_ref), custom_call_target="tpu_custom_call" | custom-call | tf_op jit(solution)/shard_map/finish_rows/pallas_call | solution.py:462
  (2 shorter events, 0.0 us)
Async XLA Ops:
  0.0 38.0 %collective-permute-start = (bf16[4,128,1024]{2,1,0:T(8,128)(2,1)}, bf16[4,128,1024]{2,1,0:T(8,128)(2,1)}, u32[]{:S(2)}, u32[]{:S(2)}) collective-permute-start(bf16[4,128,1024]{2,1,0:T(8,128)(2,1)} %refs_0_.3), channel_id=1, source_target_pairs={{8,0},{0,8},{24,16},{16,24},{9,1},{1,9},{25,17},{17,25},{10,2},{2,... | collective-permute-start | bytes 3145736 | tf_op jit(solution)/shard_map/ppermute | solution.py:380
  0.5 37.5 %collective-permute-start.1 = (bf16[4,128,1024]{2,1,0:T(8,128)(2,1)}, bf16[4,128,1024]{2,1,0:T(8,128)(2,1)}, u32[]{:S(2)}, u32[]{:S(2)}) collective-permute-start(bf16[4,128,1024]{2,1,0:T(8,128)(2,1)} %refs_0_.3), channel_id=1, source_target_pairs={{16,0},{24,8},{0,16},{8,24},{17,1},{25,9},{1,17},{9,25},{18,2},{26... | collective-permute-start | bytes 3145736 | tf_op jit(solution)/shard_map/ppermute | solution.py:382
  4.1 1.9 %copy-start = (s32[512]{0:T(512)}, s32[512]{0:T(512)S(1)}, u32[]{:S(2)}) copy-start(s32[512]{0:T(512)S(1)} %select_select_fusion) | copy-start | bytes 6148
  5.9 14.0 %copy-start.1 = (s32[32]{0:T(128)}, s32[32]{0:T(128)S(1)}, u32[]{:S(2)}) copy-start(s32[32]{0:T(128)S(1)} %select_reduce_fusion.1.slot_ref) | copy-start | bytes 388

commit v4 on v3

--- a/solution.py
+++ b/solution.py
@@ -58,7 +58,7 @@
         copy(d).wait_send()
 
 
-def sort_kernel(n, half, occ, bc, slot_ref, live_ref, *refs):
+def sort_kernel(n, half, occ, bc, slot_ref, count_ref, *refs):
     tiles, (place_ref, u_ref, w_ref, swap_ref) = refs[:bc], refs[bc:]
     i = pl.program_id(0)
     rows = place_ref.shape[2]
@@ -75,7 +75,7 @@
         o = i * (tile // rows) + j
         equal = iota((rows, rows), 0) == place_ref[o]
         for c in range(bc):
-            hit = equal & (live_ref[i * bc + c] > 0)
+            hit = equal & (slot_ref[i * bc + c] < count_ref[0])
             one_hot = hit.astype(F32).astype(BF16)
             got = jnp.dot(one_hot, tiles[c][0, 0, 0, j * rows : (j + 1) * rows, :], preferred_element_type=F32)
             at = slice(c * tile, (c + 1) * tile)
@@ -138,10 +138,8 @@
     def owner(k, of_side):
         return 2 * lax.rem(level + 1 + k, levels) + of_side
 
-    for of_side in (1 - side, side):
-        for k in range(levels):
-            for copy in load(owner(k, of_side)):
-                copy.start()
+    for copy in load(owner(0, 1 - side)):
+        copy.start()
 
     barrier = pltpu.get_barrier_semaphore()
     for d in range(1, n):
@@ -154,6 +152,12 @@
     for k in local:
         load_t(k).wait()
     load_p.wait()
+    for k in range(1, levels):
+        for copy in load(owner(k, 1 - side)):
+            copy.start()
+    for k in range(levels):
+        for copy in load(owner(k, side)):
+            copy.start()
     for k in crossed:
         swap_t(k).wait_recv()
     high = 256
@@ -330,7 +334,9 @@
                 copy.wait_send()
 
 
-def final_kernel(half, own, z_ref, swap_ref, place_ref, mirror_ref, pair_ref, occ_ref, out_ref, pieces):
+def final_kernel(
+    half, own, z_ref, swap_ref, place_ref, mirror_ref, pair_ref, occ_ref, out_ref, pieces, hot_own, hot_far, hot_self, pair_of
+):
     rows, width = z_ref.shape
 
     @pl.when(pl.program_id(0) == 0)
@@ -341,26 +347,36 @@
             pieces[p] = piece
             rest = rest - piece.astype(F32)
 
+        same = iota((rows, rows), 0) == iota((rows, rows), 1)
+
+        def column(row):
+            return jnp.sum(jnp.where(same, row, 0.0), axis=1, keepdims=True)
+
+        place = column(place_ref[...].astype(F32)).astype(I32)
+        mirror = column(mirror_ref[...].astype(F32)).astype(I32)
+        pair_of[...] = jnp.broadcast_to(column(pair_ref[...]), pair_of.shape)
+
+        def hot(out, first):
+            number = iota(out.shape, 1) + first
+            out[...] = ((number == place) | (number == mirror)).astype(F32).astype(BF16)
+
+        hot(hot_own, 0)
+        hot(hot_far, own)
+        hot(hot_self, rows)
+
     chunk = out_ref.shape[1]
     at = pl.ds(pl.multiple_of(pl.program_id(0) * chunk, chunk), chunk)
-    place, mirror = place_ref[...], mirror_ref[...]
-
-    def hot(count, first):
-        number = iota((rows, count), 1) + first
-        return ((number == place) | (number == mirror)).astype(F32).astype(BF16)
-
-    hot_own, hot_far, hot_self = hot(own, 0), hot(rows - own, own), hot(2 * half, rows)
     mixer = swap_ref[...]
     total = None
     for p in (1, 0):
         far = jnp.dot(pieces[p, own:, :], mixer, preferred_element_type=F32).astype(BF16)
         near = jnp.dot(pieces[p, : 2 * half, :], mixer, preferred_element_type=F32).astype(BF16)
-        term = jnp.dot(hot_own, pieces[p, :own, at], preferred_element_type=F32)
-        mine = jnp.dot(hot_self, near, preferred_element_type=F32)
-        other = jnp.dot(hot_far, far, preferred_element_type=F32)
+        term = jnp.dot(hot_own[...], pieces[p, :own, at], preferred_element_type=F32)
+        mine = jnp.dot(hot_self[...], near, preferred_element_type=F32)
+        other = jnp.dot(hot_far[...], far, preferred_element_type=F32)
         term = term + (mine + other)
         total = term if total is None else total + term
-    out_ref[...] = total / (pair_ref[...] - occ_ref[...])
+    out_ref[...] = total / (pair_of[:, :1] - occ_ref[...])
 
 
 def body(integrals, tile_count, tile_list, amplitudes, pair_energy, occ_energy, partner):
@@ -394,7 +410,6 @@
 
     number = jnp.arange(slots, dtype=I32)
     slot = jnp.sum(jnp.where(tile_list[0, 0][None, :] == number[:, None], number[None, :], 0), axis=1)
-    live = (slot < tile_count[0, 0]).astype(I32)
 
     per = tile // rows
 
@@ -423,7 +438,7 @@
             flops=2 * slots * rows * tile * tile, bytes_accessed=4 * slots * tile * tile, transcendentals=0
         ),
         name="sort_rows",
-    )(slot, live, *([integrals] * bc), places)
+    )(slot, tile_count.reshape(1), *([integrals] * bc), places)
 
     anywhere = pl.BlockSpec(memory_space=pl.ANY)
     wide = 256
@@ -465,18 +480,24 @@
         in_specs=[
             pl.BlockSpec((rows, width), whole),
             pl.BlockSpec((width, chunk), lambda k: (0, k)),
-            pl.BlockSpec((rows, 1), whole),
-            pl.BlockSpec((rows, 1), whole),
-            pl.BlockSpec((rows, 1), whole),
+            pl.BlockSpec((1, rows), whole),
+            pl.BlockSpec((1, rows), whole),
+            pl.BlockSpec((1, rows), whole),
             pl.BlockSpec((1, chunk), lambda k: (0, k)),
         ],
         out_specs=pl.BlockSpec((rows, chunk), lambda k: (0, k)),
         out_shape=jax.ShapeDtypeStruct((rows, width), F32),
-        scratch_shapes=[pltpu.VMEM((2, rows, width), BF16)],
+        scratch_shapes=[
+            pltpu.VMEM((2, rows, width), BF16),
+            pltpu.VMEM((rows, own), BF16),
+            pltpu.VMEM((rows, rows - own), BF16),
+            pltpu.VMEM((rows, 2 * half), BF16),
+            pltpu.VMEM((rows, 128), F32),
+        ],
         compiler_params=pltpu.CompilerParams(vmem_limit_bytes=63 * 1024 * 1024),
         name="finish_rows",
     )(
-        z, swap, place[:, None], mirror[:, None], pair_energy[:, None],
+        z, swap, place[None, :], mirror[None, :], pair_energy[None, :],
         (occ_energy[:, None] + occ_energy[None, :]).reshape(1, width),
     )
 

time: 139 us -> 134 us (0.964)
  local copies, waits for them, and re-layouts: 4.61 us -> 0.67 us
  Pallas kernels: 127 us -> 124 us
    broadcast_in_dim x3 -> x0, local copies, waits for them, and re-layouts: 3.94 us -> none  [the longest x1 1.54 us: body(): pair_energy[:, None]]
    pallas_call x1, Pallas kernels: 90.8 us -> 87.7 us  [body(): pl.pallas_call(functools.partial(reduce_kernel, n, half, ranks, wide), ou...]
  transfers between devices with their start and end apart: 2 -> 2, of which waited for: 0 -> 0; matrix products, arithmetic and copies ran while one was open for 6% -> 3% of each run, Pallas kernels for 19% -> 20%
where the time goes in v4:
time: 134 us; the launch traced here: 133 us
  Pallas kernels  124 us (93%)
  other arithmetic  3.97 us (3%)
  starting transfers between devices  3 us (2%)
    pallas_call x1, Pallas kernels, body(): pl.pallas_call(functools.partial(reduce_kernel, n, half, ranks, wide), ou...  87.7 us
    pallas_call x1, Pallas kernels, body(): pl.pallas_call(functools.partial(sort_kernel, n, half, occ, bc), grid_spe...  18.1 us
    pallas_call x1, Pallas kernels, body(): pl.pallas_call(functools.partial(final_kernel, half, own), grid=(width //...  10.5 us
    pallas_call x1, Pallas kernels, body(): pl.pallas_call(functools.partial(gather_kernel, n), out_shape=jax.ShapeDt...  8.18 us
  transfers between devices with their start and end apart: 2, of which 0 were waited for; matrix products, arithmetic and copies ran while one was open for 3% of the time, Pallas kernels for 20%

profile of v4, /device:TPU:0, one launch (start us, length us, event | category | flops | bytes accessed | tf_op | source)
XLA Modules:
  0.0 132.8 jit_solution(5938570410326248127)
XLA Ops:
  0.0 0.5 collective-permute-start
  0.5 2.5 %collective-permute-start.1 = (bf16[4,128,1024]{2,1,0:T(8,128)(2,1)}, bf16[4,128,1024]{2,1,0:T(8,128)(2,1)}, u32[]{:S(2)}, u32[]{:S(2)}) collective-permute-start(bf16[4,128,1024]{2,1,0:T(8,128)(2,1)} %refs_0_.3), channel_id=1, source_target_pairs={{16,0},{24,8},{0,16},{8,24},{17,1},{25,9},{1,17},{9,25},{18,2},{26... | collective-permute-start | bytes 3145736 | tf_op jit(solution)/shard_map/ppermute | solution.py:398
  3.0 0.7 iota_select_fusion
  3.7 0.3 convert_reduce_fusion
  4.1 0.0 copy-start
  4.1 0.8 broadcast_add_fusion
  4.9 0.2 select_reduce_fusion
  5.1 1.3 select_reduce_fusion.1.slot_ref
  6.4 0.0 copy-done
  6.4 8.2 %gather_places.1.refs_4_ = s32[8,1,512]{2,1,0:T(1,128)} custom-call(s32[1,512]{1,0:T(1,128)} %bitcast.6), custom_call_target="tpu_custom_call" | custom-call | tf_op jit(solution)/shard_map/gather_places/pallas_call | solution.py:401
  15.3 0.7 add.83.occ_ref
  15.9 0.6 add_select_fusion.5
  16.5 18.1 %sort_rows.1 = (bf16[8,288,2048]{2,1,0:T(8,128)(2,1)}, bf16[8,224,2048]{2,1,0:T(8,128)(2,1)}, bf16[1024,1024]{1,0:T(8,128)(2,1)}) custom-call(s32[32]{0:T(128)} %select_reduce_fusion.1.slot_ref, s32[1]{0:T(128)} %bitcast.5.count_ref, bf16[1,1,32,512,512]{4,3,2,1,0:T(8,128)(2,1)} %refs_3_.1, bf16[1,1,32,512,512]{4,3,2,1,0:T(8,128)(2,1)} %refs_3_.1, ...), custom_call_target="tpu_custom_call" | custom-call | flops 8589934592 | bytes 33554432 | tf_op jit(solution)/shard_map/sort_rows/pallas_call | solution.py:419
  34.6 0.0 collective-permute-done.refs_1_
  34.6 0.0 collective-permute-done.1.refs_2_
  34.6 87.7 %reduce_pairs.1.z_ref = f32[512,1024]{1,0:T(8,128)} custom-call(bf16[8,288,2048]{2,1,0:T(8,128)(2,1)} %get-tuple-element.8.u_hbm, bf16[8,224,2048]{2,1,0:T(8,128)(2,1)} %get-tuple-element.9.w_hbm, bf16[1024,1024]{1,0:T(8,128)(2,1)} %get-tuple-element.10.swap_hbm.swap_ref, bf16[4,128,1024]{2,1,0:T(8,128)(2,1)} %refs_0_.3, ...), custom_call_target="tpu_custom_call" | custom-call | tf_op jit(solution)/shard_map/reduce_pairs/pallas_call | solution.py:450
  122.3 10.5 %finish_rows.1 = f32[512,1024]{1,0:T(8,128)} custom-call(f32[512,1024]{1,0:T(8,128)} %reduce_pairs.1.z_ref, bf16[1024,1024]{1,0:T(8,128)(2,1)} %get-tuple-element.10.swap_hbm.swap_ref, s32[1,512]{1,0:T(1,128)} %bitcast.7, s32[1,512]{1,0:T(1,128)} %bitcast.8, f32[1,512]{1,0:T(1,128)} %bitcast.9, f32[1,1024]{1,0:T(1,128)} %add.83.occ_ref), custom_call_target="tpu_custom_call" | custom-call | tf_op jit(solution)/shard_map/finish_rows/pallas_call | solution.py:477
  (1 shorter events, 0.0 us)
Async XLA Ops:
  0.0 34.6 %collective-permute-start = (bf16[4,128,1024]{2,1,0:T(8,128)(2,1)}, bf16[4,128,1024]{2,1,0:T(8,128)(2,1)}, u32[]{:S(2)}, u32[]{:S(2)}) collective-permute-start(bf16[4,128,1024]{2,1,0:T(8,128)(2,1)} %refs_0_.3), channel_id=1, source_target_pairs={{8,0},{0,8},{24,16},{16,24},{9,1},{1,9},{25,17},{17,25},{10,2},{2,... | collective-permute-start | bytes 3145736 | tf_op jit(solution)/shard_map/ppermute | solution.py:396
  0.5 34.1 %collective-permute-start.1 = (bf16[4,128,1024]{2,1,0:T(8,128)(2,1)}, bf16[4,128,1024]{2,1,0:T(8,128)(2,1)}, u32[]{:S(2)}, u32[]{:S(2)}) collective-permute-start(bf16[4,128,1024]{2,1,0:T(8,128)(2,1)} %refs_0_.3), channel_id=1, source_target_pairs={{16,0},{24,8},{0,16},{8,24},{17,1},{25,9},{1,17},{9,25},{18,2},{26... | collective-permute-start | bytes 3145736 | tf_op jit(solution)/shard_map/ppermute | solution.py:398
  4.1 2.4 %copy-start = (s32[512]{0:T(512)}, s32[512]{0:T(512)S(1)}, u32[]{:S(2)}) copy-start(s32[512]{0:T(512)S(1)} %select_select_fusion) | copy-start | bytes 6148

commit v5 on v4

--- a/solution.py
+++ b/solution.py
@@ -74,10 +74,11 @@
     for j in range(tile // rows):
         o = i * (tile // rows) + j
         equal = iota((rows, rows), 0) == place_ref[o]
+        one_hot = equal.astype(F32).astype(BF16)
         for c in range(bc):
-            hit = equal & (slot_ref[i * bc + c] < count_ref[0])
-            one_hot = hit.astype(F32).astype(BF16)
-            got = jnp.dot(one_hot, tiles[c][0, 0, 0, j * rows : (j + 1) * rows, :], preferred_element_type=F32)
+            live = (slot_ref[i * bc + c] < count_ref[0]).astype(F32).astype(BF16)
+            part = tiles[c][0, 0, 0, j * rows : (j + 1) * rows, :] * live
+            got = jnp.dot(one_hot, part, preferred_element_type=F32)
             at = slice(c * tile, (c + 1) * tile)
             u_ref[j, :, at] = got[:own].astype(BF16)
             for d in range(1, n):

time: 134 us -> 135 us (level)
  no operation moved by 1% of the time
where the time goes in v5:
time: 135 us; the launch traced here: 133 us
  Pallas kernels  125 us (93%)
  other arithmetic  3.97 us (3%)
  starting transfers between devices  3 us (2%)
    pallas_call x1, Pallas kernels, body(): pl.pallas_call(functools.partial(reduce_kernel, n, half, ranks, wide), ou...  87.6 us
    pallas_call x1, Pallas kernels, body(): pl.pallas_call(functools.partial(sort_kernel, n, half, occ, bc), grid_spe...  18.3 us
    pallas_call x1, Pallas kernels, body(): pl.pallas_call(functools.partial(final_kernel, half, own), grid=(width //...  10.5 us
    pallas_call x1, Pallas kernels, body(): pl.pallas_call(functools.partial(gather_kernel, n), out_shape=jax.ShapeDt...  8.18 us
  transfers between devices with their start and end apart: 2, of which 0 were waited for; matrix products, arithmetic and copies ran while one was open for 3% of the time, Pallas kernels for 20%

profile of v5, /device:TPU:0, one launch (start us, length us, event | category | flops | bytes accessed | tf_op | source)
XLA Modules:
  0.0 132.9 jit_solution(1438617590325813916)
XLA Ops:
  0.0 0.5 collective-permute-start
  0.5 2.5 %collective-permute-start.1 = (bf16[4,128,1024]{2,1,0:T(8,128)(2,1)}, bf16[4,128,1024]{2,1,0:T(8,128)(2,1)}, u32[]{:S(2)}, u32[]{:S(2)}) collective-permute-start(bf16[4,128,1024]{2,1,0:T(8,128)(2,1)} %refs_0_.3), channel_id=1, source_target_pairs={{16,0},{24,8},{0,16},{8,24},{17,1},{25,9},{1,17},{9,25},{18,2},{26... | collective-permute-start | bytes 3145736 | tf_op jit(solution)/shard_map/ppermute | solution.py:399
  3.0 0.7 iota_select_fusion
  3.7 0.3 convert_reduce_fusion
  4.1 0.0 copy-start
  4.1 0.8 broadcast_add_fusion
  4.9 0.2 select_reduce_fusion
  5.1 1.3 select_reduce_fusion.1.slot_ref
  6.4 0.0 copy-done
  6.4 8.2 %gather_places.1.refs_4_ = s32[8,1,512]{2,1,0:T(1,128)} custom-call(s32[1,512]{1,0:T(1,128)} %bitcast.6), custom_call_target="tpu_custom_call" | custom-call | tf_op jit(solution)/shard_map/gather_places/pallas_call | solution.py:402
  15.3 0.7 add.83.occ_ref
  15.9 0.6 add_select_fusion.5
  16.5 18.3 %sort_rows.1 = (bf16[8,288,2048]{2,1,0:T(8,128)(2,1)}, bf16[8,224,2048]{2,1,0:T(8,128)(2,1)}, bf16[1024,1024]{1,0:T(8,128)(2,1)}) custom-call(s32[32]{0:T(128)} %select_reduce_fusion.1.slot_ref, s32[1]{0:T(128)} %bitcast.5.count_ref, bf16[1,1,32,512,512]{4,3,2,1,0:T(8,128)(2,1)} %refs_3_.1, bf16[1,1,32,512,512]{4,3,2,1,0:T(8,128)(2,1)} %refs_3_.1, ...), custom_call_target="tpu_custom_call" | custom-call | flops 8589934592 | bytes 33554432 | tf_op jit(solution)/shard_map/sort_rows/pallas_call | solution.py:420
  34.8 0.0 collective-permute-done.refs_1_
  34.8 0.0 collective-permute-done.1.refs_2_
  34.8 87.6 %reduce_pairs.1.z_ref = f32[512,1024]{1,0:T(8,128)} custom-call(bf16[8,288,2048]{2,1,0:T(8,128)(2,1)} %get-tuple-element.8.u_hbm, bf16[8,224,2048]{2,1,0:T(8,128)(2,1)} %get-tuple-element.9.w_hbm, bf16[1024,1024]{1,0:T(8,128)(2,1)} %get-tuple-element.10.swap_hbm.swap_ref, bf16[4,128,1024]{2,1,0:T(8,128)(2,1)} %refs_0_.3, ...), custom_call_target="tpu_custom_call" | custom-call | tf_op jit(solution)/shard_map/reduce_pairs/pallas_call | solution.py:451
  122.4 10.5 %finish_rows.1 = f32[512,1024]{1,0:T(8,128)} custom-call(f32[512,1024]{1,0:T(8,128)} %reduce_pairs.1.z_ref, bf16[1024,1024]{1,0:T(8,128)(2,1)} %get-tuple-element.10.swap_hbm.swap_ref, s32[1,512]{1,0:T(1,128)} %bitcast.7, s32[1,512]{1,0:T(1,128)} %bitcast.8, f32[1,512]{1,0:T(1,128)} %bitcast.9, f32[1,1024]{1,0:T(1,128)} %add.83.occ_ref), custom_call_target="tpu_custom_call" | custom-call | tf_op jit(solution)/shard_map/finish_rows/pallas_call | solution.py:478
  (1 shorter events, 0.0 us)
Async XLA Ops:
  0.0 34.8 %collective-permute-start = (bf16[4,128,1024]{2,1,0:T(8,128)(2,1)}, bf16[4,128,1024]{2,1,0:T(8,128)(2,1)}, u32[]{:S(2)}, u32[]{:S(2)}) collective-permute-start(bf16[4,128,1024]{2,1,0:T(8,128)(2,1)} %refs_0_.3), channel_id=1, source_target_pairs={{8,0},{0,8},{24,16},{16,24},{9,1},{1,9},{25,17},{17,25},{10,2},{2,... | collective-permute-start | bytes 3145736 | tf_op jit(solution)/shard_map/ppermute | solution.py:397
  0.5 34.3 %collective-permute-start.1 = (bf16[4,128,1024]{2,1,0:T(8,128)(2,1)}, bf16[4,128,1024]{2,1,0:T(8,128)(2,1)}, u32[]{:S(2)}, u32[]{:S(2)}) collective-permute-start(bf16[4,128,1024]{2,1,0:T(8,128)(2,1)} %refs_0_.3), channel_id=1, source_target_pairs={{16,0},{24,8},{0,16},{8,24},{17,1},{25,9},{1,17},{9,25},{18,2},{26... | collective-permute-start | bytes 3145736 | tf_op jit(solution)/shard_map/ppermute | solution.py:399
  4.1 2.4 %copy-start = (s32[512]{0:T(512)}, s32[512]{0:T(512)S(1)}, u32[]{:S(2)}) copy-start(s32[512]{0:T(512)S(1)} %select_select_fusion) | copy-start | bytes 6148
